TPU v7x, 32 devices: a whole 2x2x4 slice. The times are simulated.
32 devices in a mesh: ctx: 8 (over y, x, core), wt: 4 (over z).
Axes of the slice: x: 2, y: 2, z: 4, core: 2. Of those that a mesh axis runs over, the one named last changes fastest.
Arguments:
- block_in: float32 [4, 1024, 896], P('wt', 'ctx'), may hold values from -6 to 6
- cotangent: float32 [4, 1024, 896], P('wt', 'ctx'), may hold values from -12 to 12
- pairs: int32 [8], replicated, may hold values from 0 to 7, as said below
- positions: int32 [4, 1024], P('wt', 'ctx'), may hold values from 0 to 1023, as said below
- params: float32 [4, 3728096], P('wt'), may hold values from -16 to 16
- moment1: float32 [4, 3728096], P('wt', 'ctx'), may hold values from -100000 to 100000
- moment2: float32 [4, 3728096], P('wt', 'ctx'), may hold values from 0 to 10000000000, as said below
Outputs:
- block_out: float32 [4, 1024, 896], P('wt', 'ctx')
- input_grad: float32 [4, 1024, 896], P('wt', 'ctx')
- param_grad: float32 [4, 3728096], P('wt', 'ctx')
- new_params: float32 [4, 3728096], P('wt', 'ctx')
- new_moment1: float32 [4, 3728096], P('wt', 'ctx')
- new_moment2: float32 [4, 3728096], P('wt', 'ctx')
Inputs may be any that keep to these rules, and one draw needn't show every extreme that they name: a permutation of 0 to 7; context index c holds blocks pairs[c] and 15 - pairs[c] of 64 tokens of every sequence. positions equals order, the causal position that pairs gives each row. `moment2`: positive.
All inputs are finite; a program needn't handle non-finite values.
Results may differ from a plain program's by a relative error of at most 0.012.
The roundings to bfloat16 on the way count: a program that leaves them out, or rounds other values in their place, can miss the bound.
Values may be sent and summed in bfloat16 or wider, within the bound.
A program may use at most 256 MiB of HBM per device.

v0:
```python
import math

import jax
import jax.numpy as jnp
from jax import lax
from jax.sharding import PartitionSpec as P

D = 896
QUERY_HEADS = 14
KEY_VALUE_HEADS = 2
HEAD_SIZE = 64
FF = 4864
QW = 896
KEY_FEATURES = 128


theta_base = 1000000.0
norm_eps = 1e-06
beta_one = 0.9
beta_two = 0.95
adam_eps = 1e-08
learn_rate = 0.02
decay_rate = 0.1
step_count = 10.0


def piece_shapes():
    return [
        (D, 0),
        (D, QW),
        (QW, 0),
        (D, KEY_FEATURES),
        (KEY_FEATURES, 0),
        (D, KEY_FEATURES),
        (KEY_FEATURES, 0),
        (QW, D),
        (D, 0),
        (FF, D),
        (FF, D),
        (FF, D),
    ]


def shard_bounds(parts):
    bounds = [0]
    for rows_full, cols in piece_shapes():
        length = rows_full // parts
        if cols > 0:
            length = length * cols
        bounds.append(bounds[-1] + length)
    return bounds


def unpack(rows_arr, parts, first, last):
    bounds = shard_bounds(parts)
    shapes = piece_shapes()
    count = rows_arr.shape[0]
    base = bounds[first]
    result = []
    for number in range(first, last):
        rows_full, cols = shapes[number]
        piece = rows_arr[:, bounds[number] - base : bounds[number + 1] - base]
        if cols > 0:
            result.append(piece.reshape(count * (rows_full // parts), cols))
        else:
            result.append(piece.reshape(-1))
    return result


def decay_mask(index_vec, parts):
    bounds = shard_bounds(parts)
    result = jnp.zeros(index_vec.shape, jnp.float32)
    for number in (1, 3, 5, 7, 9, 10, 11):
        inside = (index_vec >= bounds[number]) & (index_vec < bounds[number + 1])
        result = result + jnp.where(inside, 1.0, 0.0).astype(jnp.float32)
    return result


def rope_tables(position):
    freq_index = jnp.arange(HEAD_SIZE // 2, dtype=jnp.float32)
    inverse = jnp.exp(freq_index * (-2.0 * math.log(theta_base) / HEAD_SIZE))
    angles = position.astype(jnp.float32)[:, None] * inverse[None, :]
    cosine_table = jnp.cos(angles)
    sine_lookup = jnp.sin(angles)
    return (
        jnp.concatenate([cosine_table, cosine_table], 1),
        jnp.concatenate([sine_lookup, sine_lookup], 1),
    )


def rotary_apply(values, cosine_table, sine_lookup):
    top_half = values[..., HEAD_SIZE // 2 :]
    low_half = values[..., : HEAD_SIZE // 2]
    turned = jnp.concatenate([-top_half, low_half], -1)
    return values * cosine_table[:, None, :] + turned * sine_lookup[:, None, :]


def rotary_inverse(gradient, cosine_table, sine_lookup):
    scaled = gradient * sine_lookup[:, None, :]
    turned = jnp.concatenate([scaled[..., HEAD_SIZE // 2 :], -scaled[..., : HEAD_SIZE // 2]], -1)
    return gradient * cosine_table[:, None, :] + turned


def lookup(table, index_vec):
    slots = jnp.arange(table.shape[0], dtype=jnp.int32)
    return jnp.sum(jnp.where(index_vec[..., None] == slots, table, 0), -1)


def outer_dot(left, right):
    return lax.dot_general(
        left, right, (((0,), (0,)), ((), ())), preferred_element_type=jnp.float32
    )


def inner_dot(left, right):
    return lax.dot_general(
        left, right, (((1,), (1,)), ((), ())), preferred_element_type=jnp.float32
    )


def gate_terms(gate_pre, up_pre, d_hidden):
    sigmoid_gate = jax.nn.sigmoid(gate_pre)
    silu_gate = gate_pre * sigmoid_gate
    d_gate = (d_hidden * up_pre * sigmoid_gate * (1.0 + gate_pre * (1.0 - sigmoid_gate))).astype(
        jnp.bfloat16
    )
    d_up = (d_hidden * silu_gate).astype(jnp.bfloat16)
    return (d_gate, d_up)


def hidden_units(gate_pre, up_pre):
    return (gate_pre * jax.nn.sigmoid(gate_pre) * up_pre).astype(jnp.bfloat16)


def body(block_in, cotangent, pairs, positions, params, moment1, moment2):
    n_ctx = lax.axis_size("ctx")
    n_wt = lax.axis_size("wt")
    token_rows = block_in.shape[1]
    half_rows = token_rows // 2
    seq_len = token_rows * n_ctx
    key_tile = min(512, seq_len)
    query_group_width = QUERY_HEADS // KEY_VALUE_HEADS
    score_scale = 1.0 / math.sqrt(HEAD_SIZE)
    ctx_id = lax.axis_index("ctx")
    wt_id = lax.axis_index("wt")
    x_rows = block_in[0]
    cot_rows = cotangent[0]
    row_bf = params.astype(jnp.bfloat16)
    prefix = shard_bounds(n_wt)[9]
    attn_all = lax.all_gather(row_bf[:, :prefix], "wt", axis=0, tiled=True)
    gain_b, wq_b, bq_b, wk_b, bk_b, wv_b, bv_b, wo_b, gain_two = unpack(attn_all, n_wt, 0, 9)
    gain_full = gain_b.astype(jnp.float32)
    inv_rms = lax.rsqrt(jnp.mean(x_rows * x_rows, -1, keepdims=True) + norm_eps)
    normed = (x_rows * inv_rms * gain_full).astype(jnp.bfloat16)
    queries = jnp.dot(normed, wq_b, preferred_element_type=jnp.float32) + bq_b.astype(jnp.float32)
    key_projected = jnp.dot(normed, wk_b, preferred_element_type=jnp.float32) + bk_b.astype(
        jnp.float32
    )
    value_projected = jnp.dot(normed, wv_b, preferred_element_type=jnp.float32) + bv_b.astype(
        jnp.float32
    )
    cosine_table, sine_lookup = rope_tables(positions[0])
    query_narrow = rotary_apply(
        queries.reshape(token_rows, QUERY_HEADS, HEAD_SIZE), cosine_table, sine_lookup
    ).astype(jnp.bfloat16)
    key_narrow = rotary_apply(
        key_projected.reshape(token_rows, KEY_VALUE_HEADS, HEAD_SIZE), cosine_table, sine_lookup
    ).astype(jnp.bfloat16)
    value_narrow = value_projected.astype(jnp.bfloat16)
    own_kv = jnp.concatenate([key_narrow.reshape(token_rows, KEY_FEATURES), value_narrow], 1)
    all_kv = lax.all_gather(own_kv, "ctx", axis=0, tiled=True)
    block_ids = jnp.arange(2 * n_ctx, dtype=jnp.int32)
    target = jnp.where(block_ids < n_ctx, block_ids, 2 * n_ctx - 1 - block_ids)
    owner = jnp.sum(
        jnp.where(
            pairs[None, :] == target[:, None], jnp.arange(n_ctx, dtype=jnp.int32)[None, :], 0
        ),
        1,
    )
    late_side = (block_ids >= n_ctx).astype(jnp.int32)
    causal_ids = jnp.arange(seq_len, dtype=jnp.int32)
    block_of = causal_ids // half_rows
    source_row = (
        lookup(owner, block_of) * token_rows
        + lookup(late_side, block_of) * half_rows
        + causal_ids % half_rows
    )
    sorted_kv = jnp.take(all_kv, source_row, axis=0)
    early_block = lookup(pairs, ctx_id)
    late_block = 2 * n_ctx - 1 - early_block

    def query_positions(block_now):
        return block_now * half_rows + jnp.arange(half_rows, dtype=jnp.int32)

    def tile_total(block_now):
        return ((block_now + 1) * half_rows + key_tile - 1) // key_tile

    def key_slice(tile_no):
        tile_start = tile_no * key_tile
        key_value_tile = lax.dynamic_slice_in_dim(sorted_kv, tile_start, key_tile, 0)
        key_block_tile = key_value_tile[:, :KEY_FEATURES].reshape(
            key_tile, KEY_VALUE_HEADS, HEAD_SIZE
        )
        value_tile = key_value_tile[:, KEY_FEATURES:].reshape(key_tile, KEY_VALUE_HEADS, HEAD_SIZE)
        k_pos = tile_start + jnp.arange(key_tile, dtype=jnp.int32)
        return (tile_start, key_block_tile, value_tile, k_pos)

    def attend(query_half, block_now):
        q_pos = query_positions(block_now)
        query_group = query_half.reshape(half_rows, KEY_VALUE_HEADS, query_group_width, HEAD_SIZE)

        def tile_scores(tile_no):
            tile_start, key_block_tile, value_tile, k_pos = key_slice(tile_no)
            scores = score_scale * jnp.einsum(
                "qkgd,tkd->kgqt", query_group, key_block_tile, preferred_element_type=jnp.float32
            )
            visible = k_pos[None, :] <= q_pos[:, None]
            return (jnp.where(visible, scores, -jnp.inf), value_tile)

        def total_step(tile_no, state_carry):
            run_peak, run_total = state_carry
            scores, value_tile = tile_scores(tile_no)
            new_peak = jnp.maximum(run_peak, jnp.max(scores, -1))
            factor = jnp.exp(run_peak - new_peak)
            run_total = run_total * factor + jnp.sum(jnp.exp(scores - new_peak[..., None]), -1)
            return (new_peak, run_total)

        tile_count = tile_total(block_now)
        initial_state = (
            jnp.full((KEY_VALUE_HEADS, query_group_width, half_rows), -jnp.inf, jnp.float32),
            jnp.zeros((KEY_VALUE_HEADS, query_group_width, half_rows), jnp.float32),
        )
        run_peak, run_total = lax.fori_loop(0, tile_count, total_step, initial_state)
        log_total = run_peak + jnp.log(run_total)

        def value_step(tile_no, run_accum):
            scores, value_tile = tile_scores(tile_no)
            prob_bf = jnp.exp(scores - log_total[..., None]).astype(jnp.bfloat16)
            return run_accum + jnp.einsum(
                "kgqt,tkd->kgqd", prob_bf, value_tile, preferred_element_type=jnp.float32
            )

        run_accum = lax.fori_loop(
            0,
            tile_count,
            value_step,
            jnp.zeros((KEY_VALUE_HEADS, query_group_width, half_rows, HEAD_SIZE), jnp.float32),
        )
        context_half = jnp.transpose(run_accum, (2, 0, 1, 3)).reshape(half_rows, QW)
        return (context_half, log_total)

    query_flat = query_narrow.reshape(token_rows, QW)
    ctx_early, lse_early = attend(query_flat[:half_rows], early_block)
    ctx_late, lse_late = attend(query_flat[half_rows:], late_block)
    context_rows = jnp.concatenate([ctx_early, ctx_late], 0)
    context_bf = context_rows.astype(jnp.bfloat16)
    feature_cols, context_cols = (
        lax.all_to_all(normed, "wt", split_axis=1, concat_axis=0, tiled=True),
        lax.all_to_all(context_bf, "wt", split_axis=1, concat_axis=0, tiled=True),
    )
    mid_rows = x_rows + jnp.dot(context_bf, wo_b, preferred_element_type=jnp.float32)
    gain_two_full = gain_two.astype(jnp.float32)
    inv_rms_two = lax.rsqrt(jnp.mean(mid_rows * mid_rows, -1, keepdims=True) + norm_eps)
    normed_two = (mid_rows * inv_rms_two * gain_two_full).astype(jnp.bfloat16)
    cot_bf = cot_rows.astype(jnp.bfloat16)
    normed_group, cot_group = (
        lax.all_gather(normed_two, "wt", axis=0, tiled=True),
        lax.all_gather(cot_bf, "wt", axis=0, tiled=True),
    )
    wg_own, wu_own, wd_own = unpack(row_bf[:, prefix:], n_wt, 9, 12)
    gate_pre = inner_dot(normed_group, wg_own)
    up_pre = inner_dot(normed_group, wu_own)
    hidden_bf = hidden_units(gate_pre, up_pre)
    ff_sum = lax.psum_scatter(
        jnp.dot(hidden_bf, wd_own, preferred_element_type=jnp.float32),
        "wt",
        scatter_dimension=0,
        tiled=True,
    )
    d_hidden = inner_dot(cot_group, wd_own)
    d_gate, d_up = gate_terms(gate_pre, up_pre, d_hidden)
    grad_wg = outer_dot(d_gate, normed_group)
    grad_wu = outer_dot(d_up, normed_group)
    grad_wd = outer_dot(hidden_bf, cot_group)
    d_norm_two = lax.psum_scatter(
        jnp.dot(d_gate, wg_own, preferred_element_type=jnp.float32)
        + jnp.dot(d_up, wu_own, preferred_element_type=jnp.float32),
        "wt",
        scatter_dimension=0,
        tiled=True,
    )
    block_out = mid_rows + ff_sum
    grad_gain_two = jnp.sum(d_norm_two * mid_rows * inv_rms_two, 0)
    d_scaled_two = d_norm_two * gain_two_full
    d_mid = (
        cot_rows
        + inv_rms_two * d_scaled_two
        - mid_rows
        * (inv_rms_two * inv_rms_two * inv_rms_two)
        * jnp.mean(d_scaled_two * mid_rows, -1, keepdims=True)
    )
    d_mid_bf = d_mid.astype(jnp.bfloat16)
    context_gradient = inner_dot(d_mid_bf, wo_b)
    context_gradient_narrow = context_gradient.astype(jnp.bfloat16)
    delta_rows = jnp.sum(
        (context_gradient * context_rows).reshape(
            token_rows, KEY_VALUE_HEADS, query_group_width, HEAD_SIZE
        ),
        -1,
    )

    def attend_back(query_half, half_gradient, lse_half, delta_half, block_now, key_gradients):
        q_pos = query_positions(block_now)
        query_group = query_half.reshape(half_rows, KEY_VALUE_HEADS, query_group_width, HEAD_SIZE)
        group_gradient = half_gradient.reshape(
            half_rows, KEY_VALUE_HEADS, query_group_width, HEAD_SIZE
        )
        delta_t = jnp.transpose(delta_half, (1, 2, 0))[..., None]

        def tile_step(tile_no, state_carry):
            d_query, key_gradients = state_carry
            tile_start, key_block_tile, value_tile, k_pos = key_slice(tile_no)
            scores = score_scale * jnp.einsum(
                "qkgd,tkd->kgqt", query_group, key_block_tile, preferred_element_type=jnp.float32
            )
            visible = k_pos[None, :] <= q_pos[:, None]
            scores = jnp.where(visible, scores, -jnp.inf)
            prob_tile = jnp.where(visible, jnp.exp(scores - lse_half[..., None]), 0.0)
            prob_bf = prob_tile.astype(jnp.bfloat16)
            d_probs = jnp.einsum(
                "qkgd,tkd->kgqt", group_gradient, value_tile, preferred_element_type=jnp.float32
            )
            d_scores = (prob_tile * (d_probs - delta_t)).astype(jnp.bfloat16)
            d_query = d_query + score_scale * jnp.einsum(
                "kgqt,tkd->qkgd", d_scores, key_block_tile, preferred_element_type=jnp.float32
            )
            key_part = score_scale * jnp.einsum(
                "kgqt,qkgd->tkd", d_scores, query_group, preferred_element_type=jnp.float32
            )
            value_part = jnp.einsum(
                "kgqt,qkgd->tkd", prob_bf, group_gradient, preferred_element_type=jnp.float32
            )
            update = jnp.concatenate(
                [
                    key_part.reshape(key_tile, KEY_FEATURES),
                    value_part.reshape(key_tile, KEY_FEATURES),
                ],
                1,
            )
            current = lax.dynamic_slice_in_dim(key_gradients, tile_start, key_tile, 0)
            key_gradients = lax.dynamic_update_slice_in_dim(
                key_gradients, current + update, tile_start, 0
            )
            return (d_query, key_gradients)

        initial_state = (
            jnp.zeros((half_rows, KEY_VALUE_HEADS, query_group_width, HEAD_SIZE), jnp.float32),
            key_gradients,
        )
        return lax.fori_loop(0, tile_total(block_now), tile_step, initial_state)

    key_gradients = jnp.zeros((seq_len, 2 * KEY_FEATURES), jnp.float32)
    dq_early, key_gradients = attend_back(
        query_flat[:half_rows],
        context_gradient_narrow[:half_rows],
        lse_early,
        delta_rows[:half_rows],
        early_block,
        key_gradients,
    )
    dq_late, key_gradients = attend_back(
        query_flat[half_rows:],
        context_gradient_narrow[half_rows:],
        lse_late,
        delta_rows[half_rows:],
        late_block,
        key_gradients,
    )
    d_query_rot = jnp.concatenate([dq_early, dq_late], 0).reshape(
        token_rows, QUERY_HEADS, HEAD_SIZE
    )
    d_query = rotary_inverse(d_query_rot, cosine_table, sine_lookup).reshape(token_rows, QW)
    row_ids = jnp.arange(seq_len, dtype=jnp.int32)
    local_ids = row_ids % token_rows
    chosen = lookup(pairs, row_ids // token_rows)
    back_block = jnp.where(local_ids < half_rows, chosen, 2 * n_ctx - 1 - chosen)
    back_index = back_block * half_rows + local_ids % half_rows
    per_device = jnp.take(key_gradients, back_index, axis=0)
    owned_gradients = lax.psum_scatter(per_device, "ctx", scatter_dimension=0, tiled=True)
    key_gradient = rotary_inverse(
        owned_gradients[:, :KEY_FEATURES].reshape(token_rows, KEY_VALUE_HEADS, HEAD_SIZE),
        cosine_table,
        sine_lookup,
    ).reshape(token_rows, KEY_FEATURES)
    value_gradient = owned_gradients[:, KEY_FEATURES:]
    dq_bf = d_query.astype(jnp.bfloat16)
    dk_bf = key_gradient.astype(jnp.bfloat16)
    dv_bf = value_gradient.astype(jnp.bfloat16)
    d_norm = inner_dot(dq_bf, wq_b) + inner_dot(dk_bf, wk_b) + inner_dot(dv_bf, wv_b)
    grad_gain = jnp.sum(d_norm * x_rows * inv_rms, 0)
    d_scaled = d_norm * gain_full
    d_input = inv_rms * d_scaled - x_rows * (inv_rms * inv_rms * inv_rms) * jnp.mean(
        d_scaled * x_rows, -1, keepdims=True
    )
    input_grad = d_mid + d_input
    mid_group, query_grads, key_grads_group, value_grads_group = (
        lax.all_gather(d_mid_bf, "wt", axis=0, tiled=True),
        lax.all_gather(dq_bf, "wt", axis=0, tiled=True),
        lax.all_gather(dk_bf, "wt", axis=0, tiled=True),
        lax.all_gather(dv_bf, "wt", axis=0, tiled=True),
    )
    gain_part, gain_two_part = (
        lax.psum_scatter(grad_gain, "wt", scatter_dimension=0, tiled=True),
        lax.psum_scatter(grad_gain_two, "wt", scatter_dimension=0, tiled=True),
    )
    grad_wq = outer_dot(feature_cols, query_grads)
    grad_wk = outer_dot(feature_cols, key_grads_group)
    grad_wv = outer_dot(feature_cols, value_grads_group)
    grad_wo = outer_dot(context_cols, mid_group)
    query_part = QW // n_wt
    key_part_len = KEY_FEATURES // n_wt
    bias_q = lax.dynamic_slice_in_dim(
        jnp.sum(query_grads.astype(jnp.float32), 0), wt_id * query_part, query_part, 0
    )
    bias_k = lax.dynamic_slice_in_dim(
        jnp.sum(key_grads_group.astype(jnp.float32), 0), wt_id * key_part_len, key_part_len, 0
    )
    bias_v = lax.dynamic_slice_in_dim(
        jnp.sum(value_grads_group.astype(jnp.float32), 0), wt_id * key_part_len, key_part_len, 0
    )
    shard_grad = jnp.concatenate(
        [
            gain_part,
            grad_wq.reshape(-1),
            bias_q,
            grad_wk.reshape(-1),
            bias_k,
            grad_wv.reshape(-1),
            bias_v,
            grad_wo.reshape(-1),
            gain_two_part,
            grad_wg.reshape(-1),
            grad_wu.reshape(-1),
            grad_wd.reshape(-1),
        ]
    )
    grad_piece = lax.psum_scatter(shard_grad, "ctx", scatter_dimension=0, tiled=True)
    piece_len = moment1.shape[1]
    param_grad = grad_piece.reshape(1, piece_len)
    piece_start = ctx_id * piece_len
    own_params = lax.dynamic_slice_in_dim(params[0], piece_start, piece_len, 0).reshape(
        1, piece_len
    )
    decay = decay_mask(piece_start + jnp.arange(piece_len, dtype=jnp.int32), n_wt).reshape(
        1, piece_len
    )
    new_moment1 = beta_one * moment1 + (1.0 - beta_one) * param_grad
    new_moment2 = beta_two * moment2 + (1.0 - beta_two) * param_grad * param_grad
    m_hat = new_moment1 / (1.0 - beta_one**step_count)
    v_hat = new_moment2 / (1.0 - beta_two**step_count)
    new_params = own_params - learn_rate * (
        m_hat / (jnp.sqrt(v_hat) + adam_eps) + decay_rate * decay * own_params
    )
    return (
        block_out.reshape(1, token_rows, D),
        input_grad.reshape(1, token_rows, D),
        param_grad,
        new_params,
        new_moment1,
        new_moment2,
    )


def solution(mesh):
    in_specs = (
        P("wt", "ctx", None),
        P("wt", "ctx", None),
        P(),
        P("wt", "ctx"),
        P("wt", None),
        P("wt", "ctx"),
        P("wt", "ctx"),
    )
    out_specs = (
        P("wt", "ctx", None),
        P("wt", "ctx", None),
        P("wt", "ctx"),
        P("wt", "ctx"),
        P("wt", "ctx"),
        P("wt", "ctx"),
    )
    return jax.shard_map(body, mesh=mesh, in_specs=in_specs, out_specs=out_specs, check_vma=False)
```

profile of v0, /device:TPU:0, one launch (start us, length us, event | category | flops | bytes accessed | tf_op | source)
XLA Modules:
  0.0 831.9 jit_solution(18370185866348542281)
XLA Ops:
  7.2 12.8 %convert_element_type.161 = bf16[1,3728096]{1,0:T(2,128)(2,1)S(1)} convert(f32[1,3728096]{1,0:T(1,128)} %param.23) | non-fusion elementwise | flops 3728096 | bytes 22368576 | tf_op jit(solution)/shard_map/convert_element_type | solution.py:148
  20.0 5.3 copy-done
  31.6 50.3 %slice_reduce_fusion = (bf16[1089536]{0:T(1024)(128)(2,1)S(1)}, bf16[1089536]{0:T(1024)(128)(2,1)}, bf16[1089536]{0:T(1024)(128)(2,1)}) fusion(bf16[1,3728096]{1,0:T(2,128)(2,1)} %copy-done), kind=kLoop, calls=%fused_computation.105 | loop fusion | bytes 13074432 | tf_op jit(solution)/shard_map/slice | solution.py:62
  86.9 5.0 reshape.684
  95.9 36.4 %all_gather.27 = bf16[512,896]{1,0:T(8,128)(2,1)} all-gather(bf16[128,896]{1,0:T(8,128)(2,1)S(1)} %bitcast_convert_fusion), channel_id=1, replica_groups=mesh['ctx'=8,'wt'=4] {'wt'}, dimensions={0}, use_global_device_ids=true | all-gather | bytes 1146880 | tf_op jit(solution)/shard_map/all_gather | solution.py:268
  132.3 46.2 %all-gather.3.cloned.1.call-done = bf16[4,1,459488]{2,1,0:T(2,128)(2,1)} async-done(((bf16[1,1,459488]{2,1,0:T(2,128)(2,1)}), bf16[4,1,459488]{2,1,0:T(2,128)(2,1)}) %all-gather.3.cloned.1.call-update) | async-done | bytes 3675920 | tf_op jit(solution)/shard_map/all_gather | solution.py:150
  178.5 6.7 copy.197
  191.7 9.9 %all_gather.25 = bf16[1024,256]{0,1:T(8,128)(2,1)S(1)} all-gather(bf16[128,256]{0,1:T(8,128)(2,1)S(1)} %pad_maximum_fusion.3), channel_id=1, replica_groups=mesh['ctx'=8,'wt'=4] {'ctx'}, dimensions={0}, use_global_device_ids=true | all-gather | bytes 589824 | tf_op jit(solution)/shard_map/all_gather | solution.py:171
  227.0 19.8 %all_gather.26 = bf16[512,896]{1,0:T(8,128)(2,1)S(1)} all-gather(bf16[128,896]{1,0:T(8,128)(2,1)S(1)} %multiply_convert_fusion.4), channel_id=1, replica_groups=mesh['ctx'=8,'wt'=4] {'wt'}, dimensions={0}, use_global_device_ids=true | all-gather | bytes 1146880 | tf_op jit(solution)/shard_map/all_gather | solution.py:267
  287.6 5.2 reshape.698
  297.7 5.1 reshape.699
  302.8 5.0 fusion.138
  307.8 5.2 reshape.700
  314.3 27.4 %reduce-scatter.4.cloned.1.call-done = f32[128,896]{1,0:T(8,128)} async-done(((f32[512,896]{1,0:T(8,128)}), f32[128,896]{1,0:T(8,128)}) %reduce-scatter.4.cloned.1.call-update) | async-done | bytes 458768 | tf_op jit(solution)/shard_map/reduce_scatter | solution.py:274
  349.9 5.2 while.79
  362.2 19.5 %all_gather.28 = bf16[512,896]{0,1:T(8,128)(2,1)S(1)} all-gather(bf16[128,896]{0,1:T(8,128)(2,1)S(1)} %fusion.71), channel_id=1, replica_groups=mesh['ctx'=8,'wt'=4] {'wt'}, dimensions={0}, use_global_device_ids=true | all-gather | bytes 1146880 | tf_op jit(solution)/shard_map/all_gather | solution.py:408
  387.6 22.2 %all_gather.31 = bf16[512,896]{1,0:T(8,128)(2,1)} all-gather(bf16[128,896]{1,0:T(8,128)(2,1)S(1)} %copy-done.20), channel_id=1, replica_groups=mesh['ctx'=8,'wt'=4] {'wt'}, dimensions={0}, use_global_device_ids=true | all-gather | bytes 1146880 | tf_op jit(solution)/shard_map/all_gather | solution.py:407
  418.9 12.3 %all_gather.29 = bf16[512,128]{0,1:T(8,128)(2,1)S(1)} all-gather(bf16[128,128]{0,1:T(8,128)(2,1)S(1)} %fusion.98), channel_id=1, replica_groups=mesh['ctx'=8,'wt'=4] {'wt'}, dimensions={0}, use_global_device_ids=true | all-gather | bytes 163840 | tf_op jit(solution)/shard_map/all_gather | solution.py:409
  432.6 12.4 %all_gather.30 = bf16[512,128]{0,1:T(8,128)(2,1)S(1)} all-gather(bf16[128,128]{0,1:T(8,128)(2,1)S(1)} %slice.215), channel_id=1, replica_groups=mesh['ctx'=8,'wt'=4] {'wt'}, dimensions={0}, use_global_device_ids=true | all-gather | bytes 163840 | tf_op jit(solution)/shard_map/all_gather | solution.py:410
  446.3 8.5 %all-reduce.3 = (f32[896]{0:T(1024)S(1)}, f32[896]{0:T(1024)S(1)}) all-reduce(f32[896]{0:T(1024)S(1)} %get-tuple-element.643, f32[896]{0:T(1024)S(1)} %get-tuple-element.641), channel_id=5, replica_groups=mesh['ctx'=8,'wt'=4] {'wt'}, use_global_device_ids=true, to_apply=%region_30.31.clone | all-reduce | flops 1792 | bytes 14336
  457.3 125.2 %concatenate.62 = f32[3728096]{0:T(1024)} concatenate(f32[224]{0:T(256)S(1)} %dynamic-slice.2, f32[200704]{0:T(1024)S(1)} %copy-done.14, f32[224]{0:T(256)S(1)} %dynamic_slice.36, f32[28672]{0:T(1024)S(1)} %convolution_bitcast_fusion.3, f32[32]{0:T(128)S(1)} %dynamic_slice.37, f32[28672]{0:T(1024)S(1)} %convolution_bitcast_fusion.2, f32[32]{0:T(128)S(1)} %dynamic_slice.38, ...), dimensions={0} | concatenate | bytes 29824768 | tf_op jit(solution)/shard_map/concatenate | solution.py:431
  585.4 194.9 %all-reduce.6.cloned.1.call-done = f32[3728096]{0:T(1024)} async-done(((f32[3728096]{0:T(1024)}), f32[3728096]{0:T(1024)}) %all-reduce.6.cloned.1.call-update) | async-done | bytes 14912400
  782.4 9.5 %reshape.701 = f32[1,466012]{1,0:T(1,128)} reshape(f32[466012]{0:T(1024)S(1)} %get-tuple-element.749) | data formatting | bytes 3728096 | tf_op jit(solution)/shard_map/reshape | solution.py:449
  793.9 31.0 %multiply_subtract_fusion = (f32[1,466012]{1,0:T(1,128)}, f32[1,466012]{1,0:T(1,128)}, f32[1,466012]{1,0:T(1,128)}) fusion(f32[1,3728096]{1,0:T(1,128)} %param.23, s32[]{:T(128)S(6)} %select_n.312, s32[]{:T(128)S(6)} %mul.585, f32[466012]{0:T(1024)S(1)} %get-tuple-element.748, f32[1,466012]{1,0:T(1,128)S(1)} %copy-done.25, ...), kind=kLoop, calls=%fused_computation.124 | loop fusion | flops 22368576 | bytes 14912392 | tf_op jit(solution)/shard_map/sub | solution.py:461
  (307 shorter events, 146.4 us)
Async XLA Ops:
  7.2 171.3 %all-gather.3.cloned.1.call-start = ((), (), s32[]{:S(2)}) async-start(), calls=%async_computation.8 | async-start | bytes 9190400 | tf_op jit(solution)/shard_map/all_gather | solution.py:150
  20.0 5.3 copy-start
  25.3 3.1 copy-start.33
  28.3 284.8 %reduce-scatter.6.cloned.1.call-start = ((), (), s32[]{:S(2)}) async-start(), calls=%async_computation.6 | async-start | bytes 2293760 | tf_op jit(solution)/shard_map/reduce_scatter | solution.py:285
  91.9 3.4 copy-start.34
  91.9 3.7 copy-start.1
  91.9 3.9 copy-start.27
  190.8 11.0 %copy-start.21 = (bf16[896,128]{1,0:T(8,128)(2,1)}, bf16[896,128]{1,0:T(8,128)(2,1)S(1)}, u32[]{:S(2)}) copy-start(bf16[896,128]{1,0:T(8,128)(2,1)S(1)} %reshape.673) | copy-start | bytes 688132
  208.7 2.6 copy-start.2
  220.4 3.0 copy-start.12
  220.4 4.7 copy-start.4
  225.1 21.7 %copy-start.8 = (bf16[1216,896]{1,0:T(8,128)(2,1)S(1)}, bf16[1216,896]{1,0:T(8,128)(2,1)}, u32[]{:S(2)}) copy-start(bf16[1216,896]{1,0:T(8,128)(2,1)} %reshape.683) | copy-start | bytes 6537220
  258.6 83.1 %reduce-scatter.4.cloned.1.call-start = ((), (), s32[]{:S(2)}) async-start(), calls=%async_computation.5 | async-start | bytes 2293760 | tf_op jit(solution)/shard_map/reduce_scatter | solution.py:274
  267.7 114.0 %all-to-all-start = ((bf16[128,4,224]{0,2,1:T(8,128)(2,1)}), bf16[128,4,224]{0,2,1:T(8,128)(2,1)}, u32[]{:S(2)}, u32[]{:S(2)}) async-start(bf16[128,4,224]{0,2,1:T(8,128)(2,1)} %multiply_convert_fusion.3), calls=%async_computation.3 | async-start | bytes 458752 | tf_op jit(solution)/shard_map/all_to_all | solution.py:258
  271.8 145.3 %reduce-scatter.8.cloned.1.call-start = ((), (), s32[]{:S(2)}) async-start(), calls=%async_computation.7 | async-start | bytes 1179648 | tf_op jit(solution)/shard_map/reduce_scatter | solution.py:389
  346.1 3.6 copy-start.31
  381.7 28.1 %all-to-all-start.1 = ((bf16[128,4,224]{0,2,1:T(8,128)(2,1)}), bf16[128,4,224]{0,2,1:T(8,128)(2,1)S(1)}, u32[]{:S(2)}, u32[]{:S(2)}) async-start(bf16[128,4,224]{0,2,1:T(8,128)(2,1)} %copy.155), calls=%async_computation.4 | async-start | bytes 458752 | tf_op jit(solution)/shard_map/all_to_all | solution.py:259
  385.1 395.2 %all-reduce.6.cloned.1.call-start = ((), (), s32[]{:S(2)}) async-start(), calls=%async_computation.9 | async-start | bytes 29827072
  409.8 5.0 copy-start.3
  414.5 16.7 %copy-start.22 = (bf16[896,128]{1,0:T(8,128)(2,1)S(1)}, bf16[896,128]{1,0:T(8,128)(2,1)}, u32[]{:S(2)}) copy-start(bf16[896,128]{1,0:T(8,128)(2,1)} %copy-done.21) | copy-start | bytes 688132
  417.1 28.2 %copy-start.24 = (bf16[896,128]{1,0:T(8,128)(2,1)S(1)}, bf16[896,128]{1,0:T(8,128)(2,1)}, u32[]{:S(2)}) copy-start(bf16[896,128]{1,0:T(8,128)(2,1)} %copy-done.23) | copy-start | bytes 688132
  417.1 15.5 %copy-start.32 = (f32[128,256]{0,1:T(8,128)S(1)}, f32[128,256]{0,1:T(8,128)}, u32[]{:S(2)}) copy-start(f32[128,256]{0,1:T(8,128)} %reduce-scatter.8.cloned.1.call-done) | copy-start | bytes 393220
  432.5 24.8 %copy-start.14 = (f32[200704]{0:T(1024)S(1)}, f32[200704]{0:T(1024)}, u32[]{:S(2)}) copy-start(f32[200704]{0:T(1024)} %reshape.694) | copy-start | bytes 2408452
  432.5 24.8 %copy-start.15 = (f32[200704]{0:T(1024)S(1)}, f32[200704]{0:T(1024)}, u32[]{:S(2)}) copy-start(f32[200704]{0:T(1024)} %reshape.697) | copy-start | bytes 2408452
  (20 other events, 30.5 us)
Sparse Core Ops, SparseCore 0:
  28.4 150.0 all-gather.2
  258.7 41.1 reduce-scatter.5
  302.8 38.7 reduce-scatter.3
  361.4 35.1 reduce-scatter.7
  582.7 197.5 all-reduce.5
where the time goes:
time: 849 us; the launch traced here: 832 us
  local copies, waits for them, and re-layouts  272 us (32%)
  waiting for transfers between devices  269 us (32%)
  blocking collectives  141 us (17%)
  other arithmetic  65.5 us (8%)
  matrix products  57.2 us (7%)
  between operations  19.1 us (2%)
    unnamed x6, waiting for transfers between devices  195 us
    concatenate x1, local copies, waits for them, and re-layouts, body(): jnp.concatenate([gain_part, grad_wq.reshape(-1), bias_q, grad_wk.reshape(...  125 us
    slice x3, local copies, waits for them, and re-layouts, unpack(): piece = rows_arr[:, bounds[number] - base:bounds[number + 1] - base]  52.9 us
    all_gather x1, waiting for transfers between devices, body(): attn_all = lax.all_gather(row_bf[:, :prefix], 'wt', axis=0, tiled=True)  46.2 us
    all_gather x1, blocking collectives, body(): lax.all_gather(cot_bf, 'wt', axis=0, tiled=True)  36.4 us
    sub x1, other arithmetic, body(): own_params - learn_rate * (m_hat / (jnp.sqrt(v_hat) + adam_eps) + decay_r...  31 us
    reduce_scatter x1, waiting for transfers between devices, body(): lax.psum_scatter(jnp.dot(hidden_bf, wd_own, preferred_element_type=jnp.fl...  27.4 us
    unnamed x85, local copies, waits for them, and re-layouts  22.7 us
  transfers between devices with their start and end apart: 7, of which 3 were waited for; matrix products, arithmetic and copies ran while one was open for 18% of the time, Pallas kernels for 0%

commit v1 on v0

--- a/solution.py
+++ b/solution.py
@@ -3,6 +3,8 @@
 import jax
 import jax.numpy as jnp
 from jax import lax
+from jax.experimental import pallas as pl
+from jax.experimental.pallas import tpu as pltpu
 from jax.sharding import PartitionSpec as P
 
 D = 896
@@ -132,6 +134,200 @@
     return (gate_pre * jax.nn.sigmoid(gate_pre) * up_pre).astype(jnp.bfloat16)
 
 
+LANES = 128
+COLUMN_TILES = D // LANES
+VMEM_BYTES = 56 * 1024 * 1024
+MATRIX_COLS = QW + 2 * KEY_FEATURES + D
+
+
+def big_pieces(parts):
+    bounds = shard_bounds(parts)
+    row_count = D // parts
+    return [
+        (bounds[1], row_count, COLUMN_TILES, 0),
+        (bounds[3], row_count, 1, QW),
+        (bounds[5], row_count, 1, QW + KEY_FEATURES),
+        (bounds[7], row_count, COLUMN_TILES, QW + 2 * KEY_FEATURES),
+    ]
+
+
+def chunk_rows(rows):
+    return 32 if rows % 32 == 0 else 16
+
+
+def lane_ids(rows):
+    return lax.broadcasted_iota(jnp.int32, (rows, LANES), 1)
+
+
+def unpack_kernel(parts, flat_ref, attn_ref, wg_ref, wu_ref, wd_ref, held):
+    bounds = shard_bounds(parts)
+
+    def extract(base, rows, tiles, out_ref, column):
+        step = chunk_rows(rows)
+        flat_rows = step * tiles
+        first, lane = base // LANES, base % LANES
+
+        def chunk(number, carry):
+            at = first + number * flat_rows
+            if lane:
+                low = pltpu.roll(flat_ref[pl.ds(at, flat_rows), :], LANES - lane, 1)
+                high = pltpu.roll(flat_ref[pl.ds(at + 1, flat_rows), :], LANES - lane, 1)
+                block = jnp.where(lane_ids(flat_rows) < LANES - lane, low, high)
+            else:
+                block = flat_ref[pl.ds(at, flat_rows), :]
+            out_rows = pl.ds(pl.multiple_of(number * step, step), step)
+            if tiles == 1:
+                out_ref[out_rows, column : column + LANES] = block.astype(jnp.bfloat16)
+            else:
+                held[0:flat_rows, :] = block
+                for tile in range(tiles):
+                    part = held[pl.ds(tile, step, stride=tiles), :]
+                    left = column + tile * LANES
+                    out_ref[out_rows, left : left + LANES] = part.astype(jnp.bfloat16)
+            return carry
+
+        lax.fori_loop(0, rows // step, chunk, 0)
+
+    for base, rows, tiles, column in big_pieces(parts):
+        extract(base, rows, tiles, attn_ref, column)
+    for number, out_ref in ((9, wg_ref), (10, wu_ref), (11, wd_ref)):
+        extract(bounds[number], FF // parts, COLUMN_TILES, out_ref, 0)
+
+
+def unpack_weights(flat_rows, parts):
+    whole = pl.BlockSpec(memory_space=pltpu.VMEM)
+    ff_rows = FF // parts
+    return pl.pallas_call(
+        lambda *refs: unpack_kernel(parts, *refs),
+        out_shape=(
+            jax.ShapeDtypeStruct((D // parts, MATRIX_COLS), jnp.bfloat16),
+            jax.ShapeDtypeStruct((ff_rows, D), jnp.bfloat16),
+            jax.ShapeDtypeStruct((ff_rows, D), jnp.bfloat16),
+            jax.ShapeDtypeStruct((ff_rows, D), jnp.bfloat16),
+        ),
+        in_specs=[whole],
+        out_specs=(whole,) * 4,
+        scratch_shapes=[pltpu.VMEM((32 * COLUMN_TILES, LANES), jnp.float32)],
+        compiler_params=pltpu.CompilerParams(vmem_limit_bytes=VMEM_BYTES),
+    )(flat_rows)
+
+
+def small_rows(vectors, bases):
+    rows = []
+    where_rows = []
+    for vector, base in zip(vectors, bases):
+        lane = base % LANES
+        end = lane + vector.shape[0]
+        padded = jnp.pad(vector, (lane, -end % LANES)).reshape(-1, LANES)
+        for extra in range(padded.shape[0]):
+            where_rows.append(base // LANES + extra)
+        rows.append(padded)
+    stacked = jnp.concatenate(rows, 0)
+    return jnp.pad(stacked, ((0, -stacked.shape[0] % 8), (0, 0))), where_rows
+
+
+def ff_first_row(ctx_id, piece_len, prefix, total_rows, taken):
+    rows = [
+        min(max(0, (number * piece_len - prefix) // D // 16 * 16), total_rows - taken)
+        for number in range(ctx_id)
+    ]
+    return rows
+
+
+def assemble_kernel(
+    parts, row_of_small, place_ref, small_ref, attn_ref, terms_ref, own_ref, grad_ref, param_ref,
+    flat, held,
+):
+    senders, taken = terms_ref.shape[0], terms_ref.shape[1]
+    prefix = shard_bounds(parts)[9]
+    out_rows = grad_ref.shape[0]
+    prefix_rows = prefix // LANES + 2
+    flat[0:prefix_rows, :] = jnp.zeros((prefix_rows, LANES), jnp.float32)
+    for number, row in enumerate(row_of_small):
+        flat[row : row + 1, :] = flat[row : row + 1, :] + small_ref[number : number + 1, :]
+
+    def insert(base, rows, tiles, load):
+        step = 16
+        flat_rows = step * tiles
+        first, lane = base // LANES, base % LANES
+
+        def chunk(number, carry):
+            at = first + number * flat_rows
+            for tile in range(tiles):
+                part = load(pl.multiple_of(number * step, step), step, tile)
+                if tiles == 1:
+                    held[0:step, :] = part
+                else:
+                    held[pl.ds(tile, step, stride=tiles), :] = part
+            block = held[0:flat_rows, :]
+            if lane:
+                block = pltpu.roll(block, lane, 1)
+                ids = lane_ids(flat_rows)
+                old = flat[pl.ds(at, flat_rows), :]
+                flat[pl.ds(at, flat_rows), :] = jnp.where(ids < lane, old, block)
+                old = flat[pl.ds(at + 1, flat_rows), :]
+                flat[pl.ds(at + 1, flat_rows), :] = jnp.where(ids < lane, block, old)
+            else:
+                flat[pl.ds(at, flat_rows), :] = block
+            return carry
+
+        lax.fori_loop(0, rows // step, chunk, 0)
+
+    def from_attn(column):
+        def load(row, count, tile):
+            left = column + tile * LANES
+            return attn_ref[pl.ds(row, count), left : left + LANES]
+
+        return load
+
+    def from_terms(row, count, tile):
+        columns = slice(tile * LANES, tile * LANES + LANES)
+        total = terms_ref[0, pl.ds(row, count), columns].astype(jnp.float32)
+        for sender in range(1, senders):
+            total = total + terms_ref[sender, pl.ds(row, count), columns].astype(jnp.float32)
+        return total
+
+    for base, rows, tiles, column in big_pieces(parts):
+        insert(base, rows, tiles, from_attn(column))
+    insert(prefix, taken, COLUMN_TILES, from_terms)
+
+    def shift(source, row_start, lane, out_ref):
+        step = 64
+        turn = (LANES - lane) % LANES
+
+        def chunk(number, carry):
+            at = row_start + number * step
+            low = pltpu.roll(source[pl.ds(at, step), :], turn, 1)
+            high = pltpu.roll(source[pl.ds(at + 1, step), :], turn, 1)
+            out_ref[pl.ds(pl.multiple_of(number * step, step), step), :] = jnp.where(
+                lane_ids(step) < LANES - lane, low, high
+            )
+            return carry
+
+        lax.fori_loop(0, out_rows // step, chunk, 0)
+
+    shift(flat, place_ref[0], place_ref[1], grad_ref)
+    shift(own_ref, place_ref[2], place_ref[3], param_ref)
+
+
+def assemble(parts, small, row_of_small, attn_sum, terms, own_rows, place, out_rows):
+    whole = pl.BlockSpec(memory_space=pltpu.VMEM)
+    prefix = shard_bounds(parts)[9]
+    flat_rows = prefix // LANES + terms.shape[1] * COLUMN_TILES + out_rows // 8 * 8 + 80
+    shape = jax.ShapeDtypeStruct((out_rows, LANES), jnp.float32)
+    return pl.pallas_call(
+        lambda *refs: assemble_kernel(parts, row_of_small, *refs),
+        out_shape=(shape, shape),
+        in_specs=[pl.BlockSpec(memory_space=pltpu.SMEM)] + [whole] * 4,
+        out_specs=(whole, whole),
+        scratch_shapes=[
+            pltpu.VMEM((flat_rows, LANES), jnp.float32),
+            pltpu.VMEM((16 * COLUMN_TILES, LANES), jnp.float32),
+        ],
+        compiler_params=pltpu.CompilerParams(vmem_limit_bytes=VMEM_BYTES),
+    )(place, small, attn_sum, terms, own_rows)
+
+
 def body(block_in, cotangent, pairs, positions, params, moment1, moment2):
     n_ctx = lax.axis_size("ctx")
     n_wt = lax.axis_size("wt")
@@ -145,10 +341,28 @@
     wt_id = lax.axis_index("wt")
     x_rows = block_in[0]
     cot_rows = cotangent[0]
-    row_bf = params.astype(jnp.bfloat16)
-    prefix = shard_bounds(n_wt)[9]
-    attn_all = lax.all_gather(row_bf[:, :prefix], "wt", axis=0, tiled=True)
-    gain_b, wq_b, bq_b, wk_b, bk_b, wv_b, bv_b, wo_b, gain_two = unpack(attn_all, n_wt, 0, 9)
+    bounds = shard_bounds(n_wt)
+    prefix = bounds[9]
+    shard_len = params.shape[1]
+    flat_params = jnp.pad(params[0], (0, -shard_len % 1024 + 10240)).reshape(-1, LANES)
+    attn_own, wg_own, wu_own, wd_own = unpack_weights(flat_params, n_wt)
+    vector_numbers = (0, 2, 4, 6, 8)
+    vectors_own = jnp.concatenate(
+        [params[0, bounds[number] : bounds[number + 1]] for number in vector_numbers]
+    ).astype(jnp.bfloat16)
+    attn_all = lax.all_gather(attn_own, "wt", axis=0, tiled=True)
+    vectors_all = lax.all_gather(vectors_own, "wt", axis=0)
+    wq_b = attn_all[:, :QW]
+    wk_b = attn_all[:, QW : QW + KEY_FEATURES]
+    wv_b = attn_all[:, QW + KEY_FEATURES : QW + 2 * KEY_FEATURES]
+    wo_b = attn_all[:, QW + 2 * KEY_FEATURES :]
+    vector_parts = []
+    left = 0
+    for number in vector_numbers:
+        width = bounds[number + 1] - bounds[number]
+        vector_parts.append(vectors_all[:, left : left + width].reshape(-1))
+        left += width
+    gain_b, bq_b, bk_b, bv_b, gain_two = vector_parts
     gain_full = gain_b.astype(jnp.float32)
     inv_rms = lax.rsqrt(jnp.mean(x_rows * x_rows, -1, keepdims=True) + norm_eps)
     normed = (x_rows * inv_rms * gain_full).astype(jnp.bfloat16)
@@ -267,7 +481,6 @@
         lax.all_gather(normed_two, "wt", axis=0, tiled=True),
         lax.all_gather(cot_bf, "wt", axis=0, tiled=True),
     )
-    wg_own, wu_own, wd_own = unpack(row_bf[:, prefix:], n_wt, 9, 12)
     gate_pre = inner_dot(normed_group, wg_own)
     up_pre = inner_dot(normed_group, wu_own)
     hidden_bf = hidden_units(gate_pre, up_pre)
@@ -279,9 +492,25 @@
     )
     d_hidden = inner_dot(cot_group, wd_own)
     d_gate, d_up = gate_terms(gate_pre, up_pre, d_hidden)
-    grad_wg = outer_dot(d_gate, normed_group)
-    grad_wu = outer_dot(d_up, normed_group)
-    grad_wd = outer_dot(hidden_bf, cot_group)
+    ff_grads = jnp.concatenate(
+        [
+            outer_dot(d_gate, normed_group).astype(jnp.bfloat16),
+            outer_dot(d_up, normed_group).astype(jnp.bfloat16),
+            outer_dot(hidden_bf, cot_group).astype(jnp.bfloat16),
+        ],
+        0,
+    )
+    piece_len = moment1.shape[1]
+    ff_rows = ff_grads.shape[0]
+    taken = min(ff_rows, (piece_len // D + 2 + 16 + 15) // 16 * 16)
+    first_rows = ff_first_row(n_ctx, piece_len, prefix, ff_rows, taken)
+    ff_terms = lax.all_to_all(
+        jnp.stack([ff_grads[row : row + taken] for row in first_rows]),
+        "ctx",
+        split_axis=0,
+        concat_axis=0,
+        tiled=True,
+    )
     d_norm_two = lax.psum_scatter(
         jnp.dot(d_gate, wg_own, preferred_element_type=jnp.float32)
         + jnp.dot(d_up, wu_own, preferred_element_type=jnp.float32),
@@ -409,48 +638,64 @@
         lax.all_gather(dk_bf, "wt", axis=0, tiled=True),
         lax.all_gather(dv_bf, "wt", axis=0, tiled=True),
     )
-    gain_part, gain_two_part = (
-        lax.psum_scatter(grad_gain, "wt", scatter_dimension=0, tiled=True),
-        lax.psum_scatter(grad_gain_two, "wt", scatter_dimension=0, tiled=True),
-    )
-    grad_wq = outer_dot(feature_cols, query_grads)
-    grad_wk = outer_dot(feature_cols, key_grads_group)
-    grad_wv = outer_dot(feature_cols, value_grads_group)
-    grad_wo = outer_dot(context_cols, mid_group)
-    query_part = QW // n_wt
-    key_part_len = KEY_FEATURES // n_wt
-    bias_q = lax.dynamic_slice_in_dim(
-        jnp.sum(query_grads.astype(jnp.float32), 0), wt_id * query_part, query_part, 0
-    )
-    bias_k = lax.dynamic_slice_in_dim(
-        jnp.sum(key_grads_group.astype(jnp.float32), 0), wt_id * key_part_len, key_part_len, 0
-    )
-    bias_v = lax.dynamic_slice_in_dim(
-        jnp.sum(value_grads_group.astype(jnp.float32), 0), wt_id * key_part_len, key_part_len, 0
-    )
-    shard_grad = jnp.concatenate(
+    attn_grads = jnp.concatenate(
         [
-            gain_part,
-            grad_wq.reshape(-1),
-            bias_q,
-            grad_wk.reshape(-1),
-            bias_k,
-            grad_wv.reshape(-1),
-            bias_v,
-            grad_wo.reshape(-1),
-            gain_two_part,
-            grad_wg.reshape(-1),
-            grad_wu.reshape(-1),
-            grad_wd.reshape(-1),
+            outer_dot(feature_cols, query_grads),
+            outer_dot(feature_cols, key_grads_group),
+            outer_dot(feature_cols, value_grads_group),
+            outer_dot(context_cols, mid_group),
+        ],
+        1,
+    ).astype(jnp.bfloat16)
+    attn_part = attn_grads.shape[0] // n_ctx
+    attn_terms = lax.all_to_all(
+        attn_grads.reshape(n_ctx, attn_part, MATRIX_COLS),
+        "ctx",
+        split_axis=0,
+        concat_axis=0,
+        tiled=True,
+    )
+    attn_sum = lax.all_gather(
+        jnp.sum(attn_terms.astype(jnp.float32), 0), "ctx", axis=0, tiled=True
+    )
+    vector_sums = lax.psum(
+        jnp.concatenate(
+            [
+                grad_gain,
+                jnp.sum(dq_bf.astype(jnp.float32), 0),
+                jnp.sum(dk_bf.astype(jnp.float32), 0),
+                jnp.sum(dv_bf.astype(jnp.float32), 0),
+                grad_gain_two,
+            ]
+        ),
+        ("ctx", "wt"),
+    )
+    small = []
+    left = 0
+    for full in (D, QW, KEY_FEATURES, KEY_FEATURES, D):
+        small.append(
+            lax.dynamic_slice_in_dim(vector_sums, left + wt_id * (full // n_wt), full // n_wt, 0)
+        )
+        left += full
+    small, row_of_small = small_rows(small, [bounds[number] for number in vector_numbers])
+    piece_start = ctx_id * piece_len
+    flat_start = piece_start - D * lookup(jnp.array(first_rows, jnp.int32), ctx_id)
+    own_row = piece_start // LANES // 8 * 8
+    out_rows = (piece_len + LANES * 64 - 1) // (LANES * 64) * 64
+    own_rows = lax.dynamic_slice_in_dim(flat_params, own_row, out_rows + 16, 0)
+    place = jnp.stack(
+        [
+            flat_start // LANES,
+            flat_start % LANES,
+            piece_start // LANES - own_row,
+            piece_start % LANES,
         ]
-    )
-    grad_piece = lax.psum_scatter(shard_grad, "ctx", scatter_dimension=0, tiled=True)
-    piece_len = moment1.shape[1]
-    param_grad = grad_piece.reshape(1, piece_len)
-    piece_start = ctx_id * piece_len
-    own_params = lax.dynamic_slice_in_dim(params[0], piece_start, piece_len, 0).reshape(
-        1, piece_len
-    )
+    ).astype(jnp.int32)
+    grad_rows, param_rows = assemble(
+        n_wt, small, row_of_small, attn_sum, ff_terms, own_rows, place, out_rows
+    )
+    param_grad = grad_rows.reshape(-1)[:piece_len].reshape(1, piece_len)
+    own_params = param_rows.reshape(-1)[:piece_len].reshape(1, piece_len)
     decay = decay_mask(piece_start + jnp.arange(piece_len, dtype=jnp.int32), n_wt).reshape(
         1, piece_len
     )

time: 849 us -> 758 us (0.89)
  local copies, waits for them, and re-layouts: 272 us -> 61.6 us
  waiting for transfers between devices: 269 us -> 95.7 us
  other arithmetic: 65.5 us -> 196 us
  blocking collectives: 141 us -> 259 us
  Pallas kernels: 0 us -> 50.4 us
    unnamed x6 -> x5, waiting for transfers between devices: 195 us -> 0.08 us
    another operation x2 -> x4, other arithmetic: 2.1 us -> 158 us
    concatenate x1 -> x4, local copies, waits for them, and re-layouts: 125 us -> 1.18 us  [the longest x1 0.97 us: rotary_inverse(): jnp.concatenate([scaled[..., HEAD_SIZE // 2:], -scaled[..., :HEAD_SIZE //...]
    psum x0 -> x1, blocking collectives: none -> 117 us  [body(): lax.psum(jnp.concatenate([grad_gain, jnp.sum(dq_bf.astype(jnp.float32), 0...]
    slice x4 -> x2, local copies, waits for them, and re-layouts: 52.9 us -> 1.5 us  [body(): params[0, bounds[number]:bounds[number + 1]]]
    pallas_call x0 -> x2, Pallas kernels: none -> 50.4 us  [the longest x1 26.4 us: unpack_weights(): pl.pallas_call(lambda *refs: unpack_kernel(parts, *refs), out_shape=(jax....]
    reshape x13 -> x8, local copies, waits for them, and re-layouts: 46.5 us -> 21.6 us  [the longest x1 11 us: body(): jnp.pad(params[0], (0, -shard_len % 1024 + 10240)).reshape(-1, LANES)]
    sub x1, other arithmetic: 31 us -> 12.1 us  [body(): own_params - learn_rate * (m_hat / (jnp.sqrt(v_hat) + adam_eps) + decay_r...]
  transfers between devices with their start and end apart: 7 -> 9, of which waited for: 3 -> 6; matrix products, arithmetic and copies ran while one was open for 18% -> 7% of each run, Pallas kernels for 0% -> 0%
where the time goes in v1:
time: 758 us; the launch traced here: 748 us
  blocking collectives  259 us (34%)
  other arithmetic  196 us (26%)
  waiting for transfers between devices  95.7 us (13%)
  local copies, waits for them, and re-layouts  61.6 us (8%)
  Pallas kernels  50.4 us (7%)
  matrix products  49.7 us (7%)
  between operations  18.8 us (2%)
  starting transfers between devices  15.7 us (2%)
    another operation x3, other arithmetic  157 us
    psum x1, blocking collectives, body(): lax.psum(jnp.concatenate([grad_gain, jnp.sum(dq_bf.astype(jnp.float32), 0...  117 us
    reduce_scatter x1, waiting for transfers between devices, body(): lax.psum_scatter(jnp.dot(hidden_bf, wd_own, preferred_element_type=jnp.fl...  41.8 us
    all_gather x1, waiting for transfers between devices, body(): attn_all = lax.all_gather(attn_own, 'wt', axis=0, tiled=True)  34.3 us
    all_gather x1, blocking collectives, body(): lax.all_gather(cot_bf, 'wt', axis=0, tiled=True)  33.6 us
    pallas_call x1, Pallas kernels, unpack_weights(): pl.pallas_call(lambda *refs: unpack_kernel(parts, *refs), out_shape=(jax....  26.4 us
    pallas_call x1, Pallas kernels, assemble(): pl.pallas_call(lambda *refs: assemble_kernel(parts, row_of_small, *refs),...  23.9 us
    all_gather x1, blocking collectives, body(): lax.all_gather(d_mid_bf, 'wt', axis=0, tiled=True)  19.9 us
  transfers between devices with their start and end apart: 9, of which 6 were waited for; matrix products, arithmetic and copies ran while one was open for 7% of the time, Pallas kernels for 0%

profile of v1, /device:TPU:0, one launch (start us, length us, event | category | flops | bytes accessed | tf_op | source)
XLA Modules:
  0.0 748.2 jit_solution(3782839648629382655)
XLA Ops:
  7.2 156.9 %fusion.168 = (bf16[1,3728096]{1,0:T(2,128)(2,1)}, f32[3728096]{0:T(1024)}) fusion(f32[1,3728096]{1,0:T(1,128)} %param.24), kind=kLoop, calls=%fused_computation.340 | loop fusion | flops 3728096 | bytes 37280960 | tf_op jit(solution)/shard_map/convert.23
  164.2 11.0 %pad_bitcast_fusion.refs_0_ = f32[29208,128]{1,0:T(8,128)} fusion(f32[3728096]{0:T(1024)} %get-tuple-element.829), kind=kLoop, calls=%fused_computation.96 | loop fusion | bytes 29866880 | tf_op jit(solution)/shard_map/reshape | solution.py:347
  175.1 26.4 %shard_map.127 = (bf16[224,2048]{1,0:T(8,128)(2,1)}, bf16[1216,896]{1,0:T(8,128)(2,1)}, bf16[1216,896]{1,0:T(8,128)(2,1)}, bf16[1216,896]{1,0:T(8,128)(2,1)}) custom-call(f32[29208,128]{1,0:T(8,128)} %pad_bitcast_fusion.refs_0_), custom_call_target="tpu_custom_call" | custom-call | tf_op jit(solution)/shard_map/pallas_call | solution.py:200
  206.6 14.9 %all-gather = bf16[4,1,736]{2,1,0:T(2,128)(2,1)S(1)} all-gather(bf16[1,1,736]{2,1,0:T(2,128)(2,1)S(1)} %bitcast.542), channel_id=1, replica_groups=mesh['ctx'=8,'wt'=4] {'wt'}, dimensions={0}, use_global_device_ids=true | all-gather | bytes 7360 | tf_op jit(solution)/shard_map/all_gather | solution.py:354
  223.3 33.6 %all_gather.35 = bf16[512,896]{1,0:T(8,128)(2,1)} all-gather(bf16[128,896]{1,0:T(8,128)(2,1)S(1)} %bitcast_convert_fusion), channel_id=1, replica_groups=mesh['ctx'=8,'wt'=4] {'wt'}, dimensions={0}, use_global_device_ids=true | all-gather | bytes 1146880 | tf_op jit(solution)/shard_map/all_gather | solution.py:482
  256.9 34.3 %all-gather.5.cloned.1.call-done = bf16[896,2048]{1,0:T(8,128)(2,1)} async-done(((bf16[224,2048]{1,0:T(8,128)(2,1)}), bf16[896,2048]{1,0:T(8,128)(2,1)}) %all-gather.5.cloned.1.call-update) | async-done | bytes 3670032 | tf_op jit(solution)/shard_map/all_gather | solution.py:353
  295.8 9.9 %all_gather.33 = bf16[1024,256]{0,1:T(8,128)(2,1)S(1)} all-gather(bf16[128,256]{0,1:T(8,128)(2,1)S(1)} %pad_maximum_fusion.6), channel_id=1, replica_groups=mesh['ctx'=8,'wt'=4] {'ctx'}, dimensions={0}, use_global_device_ids=true | all-gather | bytes 589824 | tf_op jit(solution)/shard_map/all_gather | solution.py:385
  306.0 3.9 gather_fusion
  322.0 19.8 %all_gather.34 = bf16[512,896]{1,0:T(8,128)(2,1)S(1)} all-gather(bf16[128,896]{1,0:T(8,128)(2,1)S(1)} %multiply_convert_fusion.4), channel_id=1, replica_groups=mesh['ctx'=8,'wt'=4] {'wt'}, dimensions={0}, use_global_device_ids=true | all-gather | bytes 1146880 | tf_op jit(solution)/shard_map/all_gather | solution.py:481
  360.1 4.8 fusion.179
  367.1 7.5 all-to-all-done
  399.7 41.8 %reduce-scatter.4.cloned.1.call-done = f32[128,896]{1,0:T(8,128)} async-done(((f32[512,896]{1,0:T(8,128)}), f32[128,896]{1,0:T(8,128)}) %reduce-scatter.4.cloned.1.call-update) | async-done | bytes 458768 | tf_op jit(solution)/shard_map/reduce_scatter | solution.py:487
  449.4 8.2 %while.79 = (s32[]{:T(128)}, f32[64,2,7,64]{0,3,2,1:T(8,128)S(1)}, f32[1024,256]{0,1:T(8,128)S(1)}, s32[]{:T(128)}, bf16[1024,256]{0,1:T(8,128)(2,1)S(1)}, /*ind...) while((s32[]{:T(128)}, f32[64,2,7,64]{0,3,2,1:T(8,128)S(1)}, ...), condition=%wide.region_25.26_spmd.clone, body=%wide.region_24.25_spmd.clone.sunk | while | flops 297747008 | bytes 12726007 | solution.py:589
  467.1 19.5 %all_gather.36 = bf16[512,896]{1,0:T(8,128)(2,1)S(1)} all-gather(bf16[128,896]{1,0:T(8,128)(2,1)S(1)} %add_convert_fusion), channel_id=1, replica_groups=mesh['ctx'=8,'wt'=4] {'wt'}, dimensions={0}, use_global_device_ids=true | all-gather | bytes 1146880 | tf_op jit(solution)/shard_map/all_gather | solution.py:637
  487.1 19.9 %all_gather.39 = bf16[512,896]{1,0:T(8,128)(2,1)S(1)} all-gather(bf16[128,896]{1,0:T(8,128)(2,1)S(1)} %copy-done.11), channel_id=1, replica_groups=mesh['ctx'=8,'wt'=4] {'wt'}, dimensions={0}, use_global_device_ids=true | all-gather | bytes 1146880 | tf_op jit(solution)/shard_map/all_gather | solution.py:636
  509.4 12.3 %all_gather.37 = bf16[512,128]{0,1:T(8,128)(2,1)S(1)} all-gather(bf16[128,128]{0,1:T(8,128)(2,1)S(1)} %get-tuple-element.806), channel_id=1, replica_groups=mesh['ctx'=8,'wt'=4] {'wt'}, dimensions={0}, use_global_device_ids=true | all-gather | bytes 163840 | tf_op jit(solution)/shard_map/all_gather | solution.py:638
  521.9 12.3 %all_gather.38 = bf16[512,128]{0,1:T(8,128)(2,1)S(1)} all-gather(bf16[128,128]{0,1:T(8,128)(2,1)S(1)} %get-tuple-element.850), channel_id=1, replica_groups=mesh['ctx'=8,'wt'=4] {'wt'}, dimensions={0}, use_global_device_ids=true | all-gather | bytes 163840 | tf_op jit(solution)/shard_map/all_gather | solution.py:639
  545.7 8.6 %all-to-all-done.2 = bf16[8,28,2048]{2,1,0:T(8,128)(2,1)S(1)} async-done(((bf16[8,28,2048]{2,1,0:T(8,128)(2,1)}), bf16[8,28,2048]{2,1,0:T(8,128)(2,1)S(1)}, u32[]{:S(2)}, u32[]{:S(2)}) %all-to-all-start.2) | async-done | bytes 917536 | tf_op jit(solution)/shard_map/all_to_all | solution.py:651
  554.4 4.9 all-to-all-start.3
  569.6 117.1 %psum.7 = f32[2944]{0:T(1024)S(1)} all-reduce(f32[2944]{0:T(1024)S(1)} %constant_dynamic-update-slice_fusion.3), channel_id=1, replica_groups=mesh['ctx'=8,'wt'=4] {'ctx','wt'}, use_global_device_ids=true, to_apply=%region_35.36 | all-reduce | flops 2944 | bytes 23552 | tf_op jit(solution)/shard_map/psum | solution.py:661
  691.6 23.9 %shard_map.128 = (f32[3648,128]{1,0:T(8,128)}, f32[3648,128]{1,0:T(8,128)}) custom-call(s32[4]{0:T(128)} %pad_add_fusion.refs_0_, f32[16,128]{1,0:T(8,128)} %pad.33.refs_1_, f32[224,2048]{1,0:T(8,128)} %reshape.606.refs_2_, bf16[8,544,896]{2,1,0:T(8,128)(2,1)} %all-to-all-done.3.refs_3_, f32[3664,128]{1,0:T(8,128)} %constant_dynamic-slice_fusion.6.refs_4_), custom_call_target="tpu_custom_call" | custom-call | tf_op jit(solution)/shard_map/pallas_call | solution.py:318
  715.5 3.6 fusion.169
  719.6 9.5 %reshape.579 = f32[1,466012]{1,0:T(1,128)} reshape(f32[466012]{0:T(1024)S(1)} %get-tuple-element.835) | data formatting | bytes 3728096 | tf_op jit(solution)/shard_map/reshape | solution.py:697
  729.1 12.1 %multiply_subtract_fusion = (f32[1,466012]{1,0:T(1,128)}, f32[1,466012]{1,0:T(1,128)}, f32[1,466012]{1,0:T(1,128)}) fusion(f32[466012]{0:T(1024)S(1)} %get-tuple-element.837, f32[466012]{0:T(1024)S(1)} %get-tuple-element.836, f32[466012]{0:T(1024)S(1)} %get-tuple-element.834, f32[1,466012]{1,0:T(1,128)S(1)} %copy-done.13, ...), kind=kLoop, calls=%fused_computation.131 | loop fusion | flops 5126132 | bytes 16776432 | tf_op jit(solution)/shard_map/sub | solution.py:706
  (352 shorter events, 128.9 us)
Async XLA Ops:
  7.2 284.1 %all-gather.5.cloned.1.call-start = ((), (), s32[]{:S(2)}) async-start(), calls=%async_computation.7 | async-start | bytes 4587520 | tf_op jit(solution)/shard_map/all_gather | solution.py:353
  175.1 26.5 %copy-start.40 = (s32[8]{0:T(128)S(1)}, s32[8]{0:T(128)}, u32[]{:S(2)}) copy-start(s32[8]{0:T(128)} %param.22) | copy-start | bytes 100
  175.1 26.5 %copy-start.42 = (s32[8]{0:T(128)S(1)}, s32[8]{0:T(128)}, u32[]{:S(2)}) copy-start(s32[8]{0:T(128)} %constant.355.clone) | copy-start | bytes 100
  175.1 47.0 %copy-start.45 = (s32[1,128]{1,0:T(1,128)S(1)}, s32[1,128]{1,0:T(1,128)}, u32[]{:S(2)}) copy-start(s32[1,128]{1,0:T(1,128)} %param.23) | copy-start | bytes 1540
  175.1 47.3 %copy-start = (f32[1,128,896]{2,1,0:T(8,128)S(1)}, f32[1,128,896]{2,1,0:T(8,128)}, u32[]{:S(2)}) copy-start(f32[1,128,896]{2,1,0:T(8,128)} %param.20) | copy-start | bytes 1376260
  201.6 21.6 %copy-start.16 = (f32[1,128,896]{2,1,0:T(8,128)S(1)}, f32[1,128,896]{2,1,0:T(8,128)}, u32[]{:S(2)}) copy-start(f32[1,128,896]{2,1,0:T(8,128)} %param.21) | copy-start | bytes 1376260
  201.6 196.9 %reduce-scatter.6.cloned.1.call-start = ((), (), s32[]{:S(2)}) async-start(), calls=%async_computation.9 | async-start | bytes 2293760 | tf_op jit(solution)/shard_map/reduce_scatter | solution.py:514
  222.3 88.1 %copy-start.28 = (f32[128,64]{0,1:T(8,128)}, f32[128,64]{0,1:T(8,128)S(1)}, u32[]{:S(2)}) copy-start(f32[128,64]{0,1:T(8,128)S(1)} %get-tuple-element.880) | copy-start | bytes 98308
  222.3 143.2 %copy-start.21 = (f32[128,64]{0,1:T(8,128)}, f32[128,64]{0,1:T(8,128)S(1)}, u32[]{:S(2)}) copy-start(f32[128,64]{0,1:T(8,128)S(1)} %get-tuple-element.879) | copy-start | bytes 98308
  223.1 131.3 %copy-start.35 = (f32[128]{0:T(128)}, f32[128]{0:T(128)S(1)}, u32[]{:S(2)}) copy-start(f32[128]{0:T(128)S(1)} %get-tuple-element.870) | copy-start | bytes 1540
  319.2 22.6 %copy-start.44 = (bf16[1216,896]{1,0:T(8,128)(2,1)S(1)}, bf16[1216,896]{1,0:T(8,128)(2,1)}, u32[]{:S(2)}) copy-start(bf16[1216,896]{1,0:T(8,128)(2,1)} %get-tuple-element.282) | copy-start | bytes 6537220
  356.4 18.3 %all-to-all-start = ((bf16[128,4,224]{0,2,1:T(8,128)(2,1)}), bf16[128,4,224]{0,2,1:T(8,128)(2,1)S(1)}, u32[]{:S(2)}, u32[]{:S(2)}) async-start(bf16[128,4,224]{0,2,1:T(8,128)(2,1)} %multiply_convert_fusion.3), calls=%async_computation.3 | async-start | bytes 458752 | tf_op jit(solution)/shard_map/all_to_all | solution.py:472
  359.8 81.7 %reduce-scatter.4.cloned.1.call-start = ((), (), s32[]{:S(2)}) async-start(), calls=%async_computation.8 | async-start | bytes 2293760 | tf_op jit(solution)/shard_map/reduce_scatter | solution.py:487
  377.4 18.2 %all-to-all-start.1 = ((bf16[128,4,224]{0,2,1:T(8,128)(2,1)}), bf16[128,4,224]{0,2,1:T(8,128)(2,1)S(1)}, u32[]{:S(2)}, u32[]{:S(2)}) async-start(bf16[128,4,224]{0,2,1:T(8,128)(2,1)} %copy.210), calls=%async_computation.4 | async-start | bytes 458752 | tf_op jit(solution)/shard_map/all_to_all | solution.py:473
  380.8 126.7 %reduce-scatter.8.cloned.1.call-start = ((), (), s32[]{:S(2)}) async-start(), calls=%async_computation.10 | async-start | bytes 1179648 | tf_op jit(solution)/shard_map/reduce_scatter | solution.py:618
  394.4 47.1 %copy-start.17 = (f32[1,128,896]{2,1,0:T(8,128)S(1)}, f32[1,128,896]{2,1,0:T(8,128)}, u32[]{:S(2)}) copy-start(f32[1,128,896]{2,1,0:T(8,128)} %param.21) | copy-start | bytes 1376260
  394.4 47.1 %copy-start.41 = (f32[128]{0:T(128)S(1)}, f32[128]{0:T(128)}, u32[]{:S(2)}) copy-start(f32[128]{0:T(128)} %get-tuple-element.871) | copy-start | bytes 1540
  464.9 21.8 %copy-start.7 = (bf16[8,28,512]{2,1,0:T(8,128)(2,1)S(1)}, bf16[8,28,512]{2,1,0:T(8,128)(2,1)}, u32[]{:S(2)}) copy-start(bf16[8,28,512]{2,1,0:T(8,128)(2,1)} %dot_general.137) | copy-start | bytes 688132
  467.1 39.9 %copy-start.23 = (bf16[8,28,512]{2,1,0:T(8,128)(2,1)S(1)}, bf16[8,28,512]{2,1,0:T(8,128)(2,1)}, u32[]{:S(2)}) copy-start(bf16[8,28,512]{2,1,0:T(8,128)(2,1)} %dot_general.142) | copy-start | bytes 688132
  535.4 18.9 %all-to-all-start.2 = ((bf16[8,28,2048]{2,1,0:T(8,128)(2,1)}), bf16[8,28,2048]{2,1,0:T(8,128)(2,1)S(1)}, u32[]{:S(2)}, u32[]{:S(2)}) async-start(bf16[8,28,2048]{2,1,0:T(8,128)(2,1)} %pad_maximum_fusion), calls=%async_computation.5 | async-start | bytes 2097152 | tf_op jit(solution)/shard_map/all_to_all | solution.py:651
  554.4 137.3 %all-to-all-start.3 = ((bf16[8,544,896]{2,1,0:T(8,128)(2,1)}), bf16[8,544,896]{2,1,0:T(8,128)(2,1)}, u32[]{:S(2)}, u32[]{:S(2)}) async-start(bf16[8,544,896]{2,1,0:T(8,128)(2,1)} %fusion.101), calls=%async_computation.6 | async-start | bytes 15597568 | tf_op jit(solution)/shard_map/all_to_all | solution.py:507
  559.3 129.5 %all-gather.7.cloned.1.call-start = ((), (), s32[]{:S(2)}) async-start(), calls=%async_computation.11 | async-start | bytes 2359296 | tf_op jit(solution)/shard_map/all_gather | solution.py:658
  567.3 120.6 %copy-start.18 = (f32[128,896]{1,0:T(8,128)S(1)}, f32[128,896]{1,0:T(8,128)}, u32[]{:S(2)}) copy-start(f32[128,896]{1,0:T(8,128)} %get-tuple-element.808) | copy-start | bytes 1376260
  567.3 120.6 %copy-start.43 = (f32[128]{0:T(128)S(1)}, f32[128]{0:T(128)}, u32[]{:S(2)}) copy-start(f32[128]{0:T(128)} %get-tuple-element.869) | copy-start | bytes 1540
  (34 other events, 144.5 us)
Sparse Core Ops, SparseCore 0:
  201.7 89.5 all-gather.4
  353.6 44.8 reduce-scatter.5
  401.4 40.0 reduce-scatter.3
  463.7 35.2 reduce-scatter.7
  562.3 58.6 all-gather.6

commit v2 on v1

--- a/solution.py
+++ b/solution.py
@@ -159,8 +159,18 @@
     return lax.broadcasted_iota(jnp.int32, (rows, LANES), 1)
 
 
-def unpack_kernel(parts, flat_ref, attn_ref, wg_ref, wu_ref, wd_ref, held):
+def vector_rows(parts):
     bounds = shard_bounds(parts)
+    return [
+        (bounds[number] // LANES, (bounds[number + 1] - 1) // LANES + 1)
+        for number in (0, 2, 4, 6, 8)
+    ]
+
+
+def unpack_kernel(parts, flat_ref, attn_ref, wg_ref, wu_ref, wd_ref, vector_ref, held):
+    bounds = shard_bounds(parts)
+    for number, (first_row, last_row) in enumerate(vector_rows(parts)):
+        vector_ref[number, 0 : last_row - first_row, :] = flat_ref[first_row:last_row, :]
 
     def extract(base, rows, tiles, out_ref, column):
         step = chunk_rows(rows)
@@ -204,9 +214,10 @@
             jax.ShapeDtypeStruct((ff_rows, D), jnp.bfloat16),
             jax.ShapeDtypeStruct((ff_rows, D), jnp.bfloat16),
             jax.ShapeDtypeStruct((ff_rows, D), jnp.bfloat16),
+            jax.ShapeDtypeStruct((5, 8, LANES), jnp.float32),
         ),
         in_specs=[whole],
-        out_specs=(whole,) * 4,
+        out_specs=(whole,) * 5,
         scratch_shapes=[pltpu.VMEM((32 * COLUMN_TILES, LANES), jnp.float32)],
         compiler_params=pltpu.CompilerParams(vmem_limit_bytes=VMEM_BYTES),
     )(flat_rows)
@@ -328,6 +339,127 @@
     )(place, small, attn_sum, terms, own_rows)
 
 
+MESH = pl.DeviceIdType.MESH
+
+
+def exchange_kernel(
+    n_ctx, n_wt, out_ref, back_ref, ff_ref, out_sum_ref, back_sum_ref, terms_ref,
+    out_send, back_send, out_recv, back_recv, pair_recv, pair_sum,
+    out_sems, back_sems, pair_sems, chip_sems,
+):
+    me_ctx, me_wt = lax.axis_index("ctx"), lax.axis_index("wt")
+    core, chip = lax.rem(me_ctx, 2), lax.div(me_ctx, 2)
+    chips = n_ctx // 2
+    taken = terms_ref.shape[1]
+    tokens = out_sum_ref.shape[0]
+    sibling = chip * 2 + 1 - core
+
+    def copy(source, target, sems, sent, landed, device):
+        return pltpu.make_async_remote_copy(
+            src_ref=source,
+            dst_ref=target,
+            send_sem=sems.at[0, sent],
+            recv_sem=sems.at[1, landed],
+            device_id=device,
+            device_id_type=MESH,
+        )
+
+    wt_peers = [lax.rem(me_wt + step, n_wt) for step in range(1, n_wt)]
+    chip_peers = [lax.rem(chip + step, chips) for step in range(1, chips)]
+    barrier = pltpu.get_barrier_semaphore()
+    partners = [(me_ctx, peer) for peer in wt_peers] + [(sibling, me_wt)]
+    partners += [(peer * 2 + core, me_wt) for peer in chip_peers]
+    for partner in partners:
+        pl.semaphore_signal(barrier, inc=1, device_id=partner, device_id_type=MESH)
+    pl.semaphore_wait(barrier, len(partners))
+
+    def pair_copy(peer):
+        source = ff_ref.at[peer * 2 + 1 - core]
+        return copy(source, pair_recv.at[peer], pair_sems, peer, peer, (sibling, me_wt))
+
+    def wt_copy(held, landing, sems, peer, slot):
+        return copy(held.at[peer], landing.at[slot], sems, peer, slot, (me_ctx, peer))
+
+    def chip_copy(peer, slot):
+        device = (peer * 2 + core, me_wt)
+        return copy(pair_sum.at[peer], terms_ref.at[slot], chip_sems, peer, slot, device)
+
+    for peer in chip_peers + [chip]:
+        pair_copy(peer).start()
+    for source, held, landing, sems in (
+        (back_ref, back_send, back_recv, back_sems),
+        (out_ref, out_send, out_recv, out_sems),
+    ):
+        for peer in wt_peers:
+            held[peer] = source[peer].astype(jnp.bfloat16)
+            wt_copy(held, landing, sems, peer, me_wt).start()
+    for peer in chip_peers + [chip]:
+        pair_copy(peer).wait_recv()
+
+        def add(number, carry):
+            rows = pl.ds(pl.multiple_of(number * 32, 32), 32)
+            total = ff_ref[peer * 2 + core, rows, :].astype(jnp.float32)
+            total = total + pair_recv[peer, rows, :].astype(jnp.float32)
+            pair_sum[peer, rows, :] = total.astype(jnp.bfloat16)
+            return carry
+
+        lax.fori_loop(0, taken // 32, add, 0)
+        if peer is not chip:
+            chip_copy(peer, chip).start()
+    terms_ref[chip] = pair_sum[chip]
+    for source, held, landing, sems, total_ref in (
+        (back_ref, back_send, back_recv, back_sems, back_sum_ref),
+        (out_ref, out_send, out_recv, out_sems, out_sum_ref),
+    ):
+        for peer in wt_peers:
+            wt_copy(held, landing, sems, peer, peer).wait_recv()
+
+        def total_step(number, carry):
+            rows = pl.ds(pl.multiple_of(number * 16, 16), 16)
+            total = source[me_wt, rows, :]
+            for peer in wt_peers:
+                total = total + landing[peer, rows, :].astype(jnp.float32)
+            total_ref[rows, :] = total
+            return carry
+
+        lax.fori_loop(0, tokens // 16, total_step, 0)
+    for peer in chip_peers:
+        chip_copy(peer, peer).wait_recv()
+    for peer in chip_peers + [chip]:
+        pair_copy(peer).wait_send()
+    for peer in chip_peers:
+        chip_copy(peer, chip).wait_send()
+    for held, landing, sems in (
+        (back_send, back_recv, back_sems),
+        (out_send, out_recv, out_sems),
+    ):
+        for peer in wt_peers:
+            wt_copy(held, landing, sems, peer, me_wt).wait_send()
+
+
+def exchange(out_terms, back_terms, ff_chunks):
+    n_ctx, taken = ff_chunks.shape[0], ff_chunks.shape[1]
+    n_wt, tokens = out_terms.shape[0], out_terms.shape[1]
+    chips = n_ctx // 2
+    whole = pl.BlockSpec(memory_space=pltpu.VMEM)
+    rows = jax.ShapeDtypeStruct((tokens, D), jnp.float32)
+    token_slots = pltpu.VMEM((n_wt, tokens, D), jnp.bfloat16)
+    chip_slots = pltpu.VMEM((chips, taken, D), jnp.bfloat16)
+    return pl.pallas_call(
+        lambda *refs: exchange_kernel(n_ctx, n_wt, *refs),
+        out_shape=(rows, rows, jax.ShapeDtypeStruct((chips, taken, D), jnp.bfloat16)),
+        in_specs=[whole] * 3,
+        out_specs=(whole,) * 3,
+        scratch_shapes=[token_slots] * 4
+        + [chip_slots] * 2
+        + [pltpu.SemaphoreType.DMA((2, n_wt))] * 2
+        + [pltpu.SemaphoreType.DMA((2, chips))] * 2,
+        compiler_params=pltpu.CompilerParams(
+            collective_id=1, has_side_effects=True, vmem_limit_bytes=VMEM_BYTES
+        ),
+    )(out_terms, back_terms, ff_chunks)
+
+
 def body(block_in, cotangent, pairs, positions, params, moment1, moment2):
     n_ctx = lax.axis_size("ctx")
     n_wt = lax.axis_size("wt")
@@ -345,11 +477,9 @@
     prefix = bounds[9]
     shard_len = params.shape[1]
     flat_params = jnp.pad(params[0], (0, -shard_len % 1024 + 10240)).reshape(-1, LANES)
-    attn_own, wg_own, wu_own, wd_own = unpack_weights(flat_params, n_wt)
+    attn_own, wg_own, wu_own, wd_own, vector_held = unpack_weights(flat_params, n_wt)
     vector_numbers = (0, 2, 4, 6, 8)
-    vectors_own = jnp.concatenate(
-        [params[0, bounds[number] : bounds[number + 1]] for number in vector_numbers]
-    ).astype(jnp.bfloat16)
+    vectors_own = vector_held.astype(jnp.bfloat16)
     attn_all = lax.all_gather(attn_own, "wt", axis=0, tiled=True)
     vectors_all = lax.all_gather(vectors_own, "wt", axis=0)
     wq_b = attn_all[:, :QW]
@@ -357,11 +487,12 @@
     wv_b = attn_all[:, QW + KEY_FEATURES : QW + 2 * KEY_FEATURES]
     wo_b = attn_all[:, QW + 2 * KEY_FEATURES :]
     vector_parts = []
-    left = 0
-    for number in vector_numbers:
+    for place_no, number in enumerate(vector_numbers):
+        lane = bounds[number] % LANES
         width = bounds[number + 1] - bounds[number]
-        vector_parts.append(vectors_all[:, left : left + width].reshape(-1))
-        left += width
+        vector_parts.append(
+            vectors_all[:, place_no].reshape(n_wt, 8 * LANES)[:, lane : lane + width].reshape(-1)
+        )
     gain_b, bq_b, bk_b, bv_b, gain_two = vector_parts
     gain_full = gain_b.astype(jnp.float32)
     inv_rms = lax.rsqrt(jnp.mean(x_rows * x_rows, -1, keepdims=True) + norm_eps)
@@ -484,12 +615,7 @@
     gate_pre = inner_dot(normed_group, wg_own)
     up_pre = inner_dot(normed_group, wu_own)
     hidden_bf = hidden_units(gate_pre, up_pre)
-    ff_sum = lax.psum_scatter(
-        jnp.dot(hidden_bf, wd_own, preferred_element_type=jnp.float32),
-        "wt",
-        scatter_dimension=0,
-        tiled=True,
-    )
+    out_terms = jnp.dot(hidden_bf, wd_own, preferred_element_type=jnp.float32)
     d_hidden = inner_dot(cot_group, wd_own)
     d_gate, d_up = gate_terms(gate_pre, up_pre, d_hidden)
     ff_grads = jnp.concatenate(
@@ -502,21 +628,15 @@
     )
     piece_len = moment1.shape[1]
     ff_rows = ff_grads.shape[0]
-    taken = min(ff_rows, (piece_len // D + 2 + 16 + 15) // 16 * 16)
+    taken = min(ff_rows, (piece_len // D + 2 + 16 + 31) // 32 * 32)
     first_rows = ff_first_row(n_ctx, piece_len, prefix, ff_rows, taken)
-    ff_terms = lax.all_to_all(
+    back_terms = jnp.dot(d_gate, wg_own, preferred_element_type=jnp.float32) + jnp.dot(
+        d_up, wu_own, preferred_element_type=jnp.float32
+    )
+    ff_sum, d_norm_two, ff_terms = exchange(
+        out_terms.reshape(n_wt, token_rows, D),
+        back_terms.reshape(n_wt, token_rows, D),
         jnp.stack([ff_grads[row : row + taken] for row in first_rows]),
-        "ctx",
-        split_axis=0,
-        concat_axis=0,
-        tiled=True,
-    )
-    d_norm_two = lax.psum_scatter(
-        jnp.dot(d_gate, wg_own, preferred_element_type=jnp.float32)
-        + jnp.dot(d_up, wu_own, preferred_element_type=jnp.float32),
-        "wt",
-        scatter_dimension=0,
-        tiled=True,
     )
     block_out = mid_rows + ff_sum
     grad_gain_two = jnp.sum(d_norm_two * mid_rows * inv_rms_two, 0)
@@ -694,8 +814,8 @@
     grad_rows, param_rows = assemble(
         n_wt, small, row_of_small, attn_sum, ff_terms, own_rows, place, out_rows
     )
-    param_grad = grad_rows.reshape(-1)[:piece_len].reshape(1, piece_len)
-    own_params = param_rows.reshape(-1)[:piece_len].reshape(1, piece_len)
+    param_grad = grad_rows.reshape(1, -1)[:, :piece_len]
+    own_params = param_rows.reshape(1, -1)[:, :piece_len]
     decay = decay_mask(piece_start + jnp.arange(piece_len, dtype=jnp.int32), n_wt).reshape(
         1, piece_len
     )

time: 758 us -> 693 us (0.914)
  blocking collectives: 259 us -> 182 us
  Pallas kernels: 50.4 us -> 105 us
  waiting for transfers between devices: 95.7 us -> 44.6 us
  other arithmetic: 196 us -> 214 us
  local copies, waits for them, and re-layouts: 61.6 us -> 46.8 us
    unnamed x3 -> x4, other arithmetic: 2.48 us -> 163 us
    another operation x3 -> x2, other arithmetic: 157 us -> 1.46 us
    psum x1, blocking collectives: 117 us -> 38.1 us  [body(): lax.psum(jnp.concatenate([grad_gain, jnp.sum(dq_bf.astype(jnp.float32), 0...]
    pallas_call x0 -> x1, Pallas kernels: none -> 56.1 us  [exchange(): pl.pallas_call(lambda *refs: exchange_kernel(n_ctx, n_wt, *refs), out_sha...]
    reduce_scatter x2 -> x0, waiting for transfers between devices: 44 us -> none  [the longest x1 41.8 us: body(): lax.psum_scatter(jnp.dot(hidden_bf, wd_own, preferred_element_type=jnp.fl...]
    sub x1, other arithmetic: 12.1 us -> 31.4 us  [body(): own_params - learn_rate * (m_hat / (jnp.sqrt(v_hat) + adam_eps) + decay_r...]
    reshape x1 -> x0, local copies, waits for them, and re-layouts: 9.48 us -> none  [body(): param_grad = grad_rows.reshape(-1)[:piece_len].reshape(1, piece_len)]
    reduce_scatter x1, starting transfers between devices: 0.04 us -> 8.76 us  [body(): lax.psum_scatter(per_device, 'ctx', scatter_dimension=0, tiled=True)]
  transfers between devices with their start and end apart: 9 -> 6, of which waited for: 6 -> 2; matrix products, arithmetic and copies ran while one was open for 7% -> 9% of each run, Pallas kernels for 0% -> 8%
where the time goes in v2:
time: 693 us; the launch traced here: 687 us
  other arithmetic  214 us (31%)
  blocking collectives  182 us (26%)
  Pallas kernels  105 us (15%)
  matrix products  53.8 us (8%)
  local copies, waits for them, and re-layouts  46.8 us (7%)
  waiting for transfers between devices  44.6 us (6%)
  starting transfers between devices  21.9 us (3%)
  between operations  18.4 us (3%)
    unnamed x4, other arithmetic  163 us
    pallas_call x1, Pallas kernels, exchange(): pl.pallas_call(lambda *refs: exchange_kernel(n_ctx, n_wt, *refs), out_sha...  56.1 us
    psum x1, blocking collectives, body(): lax.psum(jnp.concatenate([grad_gain, jnp.sum(dq_bf.astype(jnp.float32), 0...  38.1 us
    all_gather x1, blocking collectives, body(): lax.all_gather(cot_bf, 'wt', axis=0, tiled=True)  34.9 us
    sub x1, other arithmetic, body(): own_params - learn_rate * (m_hat / (jnp.sqrt(v_hat) + adam_eps) + decay_r...  31.4 us
    all_gather x1, waiting for transfers between devices, body(): attn_all = lax.all_gather(attn_own, 'wt', axis=0, tiled=True)  30.9 us
    pallas_call x1, Pallas kernels, unpack_weights(): pl.pallas_call(lambda *refs: unpack_kernel(parts, *refs), out_shape=(jax....  26.5 us
    pallas_call x1, Pallas kernels, assemble(): pl.pallas_call(lambda *refs: assemble_kernel(parts, row_of_small, *refs),...  22.4 us
  transfers between devices with their start and end apart: 6, of which 2 were waited for; matrix products, arithmetic and copies ran while one was open for 9% of the time, Pallas kernels for 8%

profile of v2, /device:TPU:0, one launch (start us, length us, event | category | flops | bytes accessed | tf_op | source)
XLA Modules:
  0.0 687.5 jit_solution(16689083133568415328)
XLA Ops:
  7.2 160.7 %reduce.2 = f32[3728096]{0:T(1024)} reduce(f32[1,3728096]{1,0:T(1,128)} %param.24, f32[]{:T(128)} %constant.376), dimensions={0}, to_apply=%param.24.reduce_sub_computation | reduce | bytes 29824772 | tf_op args[4]
  168.0 11.0 %pad_bitcast_fusion.refs_0_ = f32[29208,128]{1,0:T(8,128)} fusion(f32[3728096]{0:T(1024)} %reduce.2), kind=kLoop, calls=%fused_computation.96 | loop fusion | bytes 29866880 | tf_op jit(solution)/shard_map/reshape | solution.py:479
  178.9 26.5 %shard_map.127 = (bf16[224,2048]{1,0:T(8,128)(2,1)}, bf16[1216,896]{1,0:T(8,128)(2,1)}, bf16[1216,896]{1,0:T(8,128)(2,1)}, bf16[1216,896]{1,0:T(8,128)(2,1)}, f32[5,8,128]{2,1,0:T(8,128)}) custom-call(f32[29208,128]{1,0:T(8,128)} %pad_bitcast_fusion.refs_0_), custom_call_target="tpu_custom_call" | custom-call | tf_op jit(solution)/shard_map/pallas_call | solution.py:210
  206.4 14.9 %all-gather = bf16[20,8,128]{2,1,0:T(8,128)(2,1)S(1)} all-gather(bf16[5,8,128]{2,1,0:T(8,128)(2,1)S(1)} %convert_element_type.178), channel_id=2, replica_groups=mesh['ctx'=8,'wt'=4] {'wt'}, dimensions={0}, use_global_device_ids=true | all-gather | bytes 51200 | tf_op jit(solution)/shard_map/all_gather | solution.py:484
  222.2 4.8 all-to-all-start
  233.4 34.9 %all_gather.38 = bf16[512,896]{1,0:T(8,128)(2,1)} all-gather(bf16[128,896]{1,0:T(8,128)(2,1)S(1)} %bitcast_convert_fusion), channel_id=1, replica_groups=mesh['ctx'=8,'wt'=4] {'wt'}, dimensions={0}, use_global_device_ids=true | all-gather | bytes 1146880 | tf_op jit(solution)/shard_map/all_gather | solution.py:613
  269.1 30.9 %all-gather.5.cloned.1.call-done = bf16[896,2048]{1,0:T(8,128)(2,1)} async-done(((bf16[224,2048]{1,0:T(8,128)(2,1)}), bf16[896,2048]{1,0:T(8,128)(2,1)}) %all-gather.5.cloned.1.call-update) | async-done | bytes 3670032 | tf_op jit(solution)/shard_map/all_gather | solution.py:483
  304.5 10.0 %all_gather.36 = bf16[1024,256]{0,1:T(8,128)(2,1)S(1)} all-gather(bf16[128,256]{0,1:T(8,128)(2,1)S(1)} %pad_maximum_fusion.6), channel_id=1, replica_groups=mesh['ctx'=8,'wt'=4] {'ctx'}, dimensions={0}, use_global_device_ids=true | all-gather | bytes 589824 | tf_op jit(solution)/shard_map/all_gather | solution.py:516
  314.7 3.9 gather_fusion
  332.4 19.8 %all_gather.37 = bf16[512,896]{1,0:T(8,128)(2,1)S(1)} all-gather(bf16[128,896]{1,0:T(8,128)(2,1)S(1)} %multiply_convert_fusion.4), channel_id=1, replica_groups=mesh['ctx'=8,'wt'=4] {'wt'}, dimensions={0}, use_global_device_ids=true | all-gather | bytes 1146880 | tf_op jit(solution)/shard_map/all_gather | solution.py:612
  372.7 4.0 all-to-all-start.1
  376.7 8.8 %reduce-scatter.2.cloned.1.call-start = ((), (), s32[]{:S(2)}) async-start(), calls=%async_computation.5 | async-start | bytes 1179648 | tf_op jit(solution)/shard_map/reduce_scatter | solution.py:738
  399.8 56.1 %shard_map.128 = (f32[128,896]{1,0:T(8,128)}, f32[128,896]{1,0:T(8,128)}, bf16[4,544,896]{2,1,0:T(8,128)(2,1)}) custom-call(f32[4,128,896]{2,1,0:T(8,128)} %bitcast.539, f32[4,128,896]{2,1,0:T(8,128)} %bitcast.557, bf16[8,544,896]{2,1,0:T(8,128)(2,1)} %fusion.90.refs_2_), custom_call_target="tpu_custom_call" | custom-call | tf_op jit(solution)/shard_map/pallas_call | solution.py:448
  462.4 4.0 while.78
  466.5 8.0 %while.79 = (s32[]{:T(128)}, f32[64,2,7,64]{0,3,2,1:T(8,128)S(1)}, f32[1024,256]{0,1:T(8,128)S(1)}, s32[]{:T(128)}, bf16[1024,256]{0,1:T(8,128)(2,1)S(1)}, /*ind...) while((s32[]{:T(128)}, f32[64,2,7,64]{0,3,2,1:T(8,128)S(1)}, ...), condition=%wide.region_23.24_spmd.clone, body=%wide.region_22.23_spmd.clone.sunk | while | flops 297747008 | bytes 12726007 | solution.py:709
  482.8 19.6 %all_gather.39 = bf16[512,896]{1,0:T(8,128)(2,1)S(1)} all-gather(bf16[128,896]{1,0:T(8,128)(2,1)S(1)} %add_convert_fusion), channel_id=1, replica_groups=mesh['ctx'=8,'wt'=4] {'wt'}, dimensions={0}, use_global_device_ids=true | all-gather | bytes 1146880 | tf_op jit(solution)/shard_map/all_gather | solution.py:757
  503.6 20.0 %all_gather.42 = bf16[512,896]{1,0:T(8,128)(2,1)S(1)} all-gather(bf16[128,896]{1,0:T(8,128)(2,1)S(1)} %copy-done.15), channel_id=1, replica_groups=mesh['ctx'=8,'wt'=4] {'wt'}, dimensions={0}, use_global_device_ids=true | all-gather | bytes 1146880 | tf_op jit(solution)/shard_map/all_gather | solution.py:756
  529.4 12.3 %all_gather.40 = bf16[512,128]{0,1:T(8,128)(2,1)S(1)} all-gather(bf16[128,128]{0,1:T(8,128)(2,1)S(1)} %get-tuple-element.767), channel_id=1, replica_groups=mesh['ctx'=8,'wt'=4] {'wt'}, dimensions={0}, use_global_device_ids=true | all-gather | bytes 163840 | tf_op jit(solution)/shard_map/all_gather | solution.py:758
  541.9 12.3 %all_gather.41 = bf16[512,128]{0,1:T(8,128)(2,1)S(1)} all-gather(bf16[128,128]{0,1:T(8,128)(2,1)S(1)} %get-tuple-element.799), channel_id=1, replica_groups=mesh['ctx'=8,'wt'=4] {'wt'}, dimensions={0}, use_global_device_ids=true | all-gather | bytes 163840 | tf_op jit(solution)/shard_map/all_gather | solution.py:759
  555.5 4.0 all-to-all-start.2
  561.2 13.7 %all-to-all-done.2 = bf16[8,28,2048]{2,1,0:T(8,128)(2,1)S(1)} async-done(((bf16[8,28,2048]{2,1,0:T(8,128)(2,1)}), bf16[8,28,2048]{2,1,0:T(8,128)(2,1)S(1)}, u32[]{:S(2)}, u32[]{:S(2)}) %all-to-all-start.2) | async-done | bytes 917536 | tf_op jit(solution)/shard_map/all_to_all | solution.py:771
  583.9 38.1 %psum.7 = f32[2944]{0:T(1024)S(1)} all-reduce(f32[2944]{0:T(1024)S(1)} %constant_dynamic-update-slice_fusion.3), channel_id=1, replica_groups=mesh['ctx'=8,'wt'=4] {'ctx','wt'}, use_global_device_ids=true, to_apply=%region_33.34 | all-reduce | flops 2944 | bytes 23552 | tf_op jit(solution)/shard_map/psum | solution.py:781
  626.8 22.4 %shard_map.129 = (f32[3648,128]{1,0:T(8,128)}, f32[3648,128]{1,0:T(8,128)}) custom-call(s32[4]{0:T(128)} %pad_add_fusion.refs_0_, f32[16,128]{1,0:T(8,128)} %pad.33.refs_1_, f32[224,2048]{1,0:T(8,128)} %reshape.655.refs_2_, bf16[4,544,896]{2,1,0:T(8,128)(2,1)} %get-tuple-element.295.refs_3_, f32[3664,128]{1,0:T(8,128)} %constant_dynamic-slice_fusion.6.refs_4_), custom_call_target="tpu_custom_call" | custom-call | tf_op jit(solution)/shard_map/pallas_call | solution.py:329
  649.3 31.4 %multiply_subtract_fusion = (f32[1,466012]{1,0:T(1,128)}, f32[1,466012]{1,0:T(1,128)}, f32[1,466012]{1,0:T(1,128)}, f32[1,466012]{1,0:T(1,128)}) fusion(f32[1,466944]{1,0:T(1,128)} %bitcast.552, s32[]{:T(128)S(6)} %mul.560, f32[1,466012]{1,0:T(1,128)S(1)} %copy-done.16, f32[1,466012]{1,0:T(1,128)S(1)} %copy-done.17, f32[1,466944]{1,0:T(1,128)} %bitcast.551), kind=kLoop, calls=%fused_computation.125 | loop fusion | flops 23766612 | bytes 14912388 | tf_op jit(solution)/shard_map/sub | solution.py:826
  (334 shorter events, 114.8 us)
Async XLA Ops:
  7.2 292.8 %all-gather.5.cloned.1.call-start = ((), (), s32[]{:S(2)}) async-start(), calls=%async_computation.4 | async-start | bytes 4587520 | tf_op jit(solution)/shard_map/all_gather | solution.py:483
  178.9 26.5 %copy-start = (f32[1,128,896]{2,1,0:T(8,128)S(1)}, f32[1,128,896]{2,1,0:T(8,128)}, u32[]{:S(2)}) copy-start(f32[1,128,896]{2,1,0:T(8,128)} %param.20) | copy-start | bytes 1376260
  205.4 21.6 %copy-start.35 = (s32[8]{0:T(128)S(1)}, s32[8]{0:T(128)}, u32[]{:S(2)}) copy-start(s32[8]{0:T(128)} %param.22) | copy-start | bytes 100
  205.4 21.6 %copy-start.36 = (s32[8]{0:T(128)S(1)}, s32[8]{0:T(128)}, u32[]{:S(2)}) copy-start(s32[8]{0:T(128)} %constant.355.clone) | copy-start | bytes 100
  205.4 25.0 %copy-start.40 = (s32[1,128]{1,0:T(1,128)S(1)}, s32[1,128]{1,0:T(1,128)}, u32[]{:S(2)}) copy-start(s32[1,128]{1,0:T(1,128)} %param.23) | copy-start | bytes 1540
  205.6 27.6 %copy-start.19 = (f32[1,128,896]{2,1,0:T(8,128)S(1)}, f32[1,128,896]{2,1,0:T(8,128)}, u32[]{:S(2)}) copy-start(f32[1,128,896]{2,1,0:T(8,128)} %param.21) | copy-start | bytes 1376260
  206.4 26.9 %copy-start.32 = (f32[128]{0:T(128)}, f32[128]{0:T(128)S(1)}, u32[]{:S(2)}) copy-start(f32[128]{0:T(128)S(1)} %get-tuple-element.819) | copy-start | bytes 1540
  222.2 46.1 %all-to-all-start = ((bf16[128,4,224]{0,2,1:T(8,128)(2,1)}), bf16[128,4,224]{0,2,1:T(8,128)(2,1)S(1)}, u32[]{:S(2)}, u32[]{:S(2)}) async-start(bf16[128,4,224]{0,2,1:T(8,128)(2,1)} %multiply_convert_fusion.3), calls=%async_computation.1 | async-start | bytes 458752 | tf_op jit(solution)/shard_map/all_to_all | solution.py:603
  330.1 22.2 %copy-start.10 = (f32[128,896]{1,0:T(8,128)}, f32[128,896]{1,0:T(8,128)S(1)}, u32[]{:S(2)}) copy-start(f32[128,896]{1,0:T(8,128)S(1)} %constant_dynamic-update-slice_fusion) | copy-start | bytes 1376260
  330.1 22.2 %copy-start.38 = (bf16[1216,896]{1,0:T(8,128)(2,1)S(1)}, bf16[1216,896]{1,0:T(8,128)(2,1)}, u32[]{:S(2)}) copy-start(bf16[1216,896]{1,0:T(8,128)(2,1)} %get-tuple-element.287) | copy-start | bytes 6537220
  332.3 21.5 %copy-start.7 = (f32[128,896]{1,0:T(8,128)}, f32[128,896]{1,0:T(8,128)S(1)}, u32[]{:S(2)}) copy-start(f32[128,896]{1,0:T(8,128)S(1)} %get-tuple-element.823) | copy-start | bytes 1376260
  372.7 150.9 %all-to-all-start.1 = ((bf16[128,4,224]{0,2,1:T(8,128)(2,1)}), bf16[128,4,224]{0,2,1:T(8,128)(2,1)}, u32[]{:S(2)}, u32[]{:S(2)}) async-start(bf16[128,4,224]{0,2,1:T(8,128)(2,1)} %copy.176), calls=%async_computation.2 | async-start | bytes 458752 | tf_op jit(solution)/shard_map/all_to_all | solution.py:604
  376.7 150.8 %reduce-scatter.2.cloned.1.call-start = ((), (), s32[]{:S(2)}) async-start(), calls=%async_computation.5 | async-start | bytes 1179648 | tf_op jit(solution)/shard_map/reduce_scatter | solution.py:738
  399.8 56.1 %copy-start.8 = (f32[128,896]{1,0:T(8,128)S(1)}, f32[128,896]{1,0:T(8,128)}, u32[]{:S(2)}) copy-start(f32[128,896]{1,0:T(8,128)} %copy-done.7) | copy-start | bytes 1376260
  399.8 57.3 %copy-start.20 = (f32[1,128,896]{2,1,0:T(8,128)S(1)}, f32[1,128,896]{2,1,0:T(8,128)}, u32[]{:S(2)}) copy-start(f32[1,128,896]{2,1,0:T(8,128)} %param.21) | copy-start | bytes 1376260
  481.5 22.1 %copy-start.15 = (bf16[128,896]{1,0:T(8,128)(2,1)S(1)}, bf16[128,896]{1,0:T(8,128)(2,1)}, u32[]{:S(2)}) copy-start(bf16[128,896]{1,0:T(8,128)(2,1)} %copy-done.14) | copy-start | bytes 688132
  527.5 26.9 %copy-start.21 = (bf16[8,28,896]{2,1,0:T(8,128)(2,1)S(1)}, bf16[8,28,896]{2,1,0:T(8,128)(2,1)}, u32[]{:S(2)}) copy-start(bf16[8,28,896]{2,1,0:T(8,128)(2,1)} %convolution_convert_fusion.4) | copy-start | bytes 1204228
  527.5 26.9 %copy-start.22 = (bf16[8,28,896]{2,1,0:T(8,128)(2,1)S(1)}, bf16[8,28,896]{2,1,0:T(8,128)(2,1)}, u32[]{:S(2)}) copy-start(bf16[8,28,896]{2,1,0:T(8,128)(2,1)} %convolution_convert_fusion.3) | copy-start | bytes 1204228
  555.5 19.4 %all-to-all-start.2 = ((bf16[8,28,2048]{2,1,0:T(8,128)(2,1)}), bf16[8,28,2048]{2,1,0:T(8,128)(2,1)S(1)}, u32[]{:S(2)}, u32[]{:S(2)}) async-start(bf16[8,28,2048]{2,1,0:T(8,128)(2,1)} %pad_maximum_fusion), calls=%async_computation.3 | async-start | bytes 2097152 | tf_op jit(solution)/shard_map/all_to_all | solution.py:771
  559.5 64.5 %all-gather.7.cloned.1.call-start = ((), (), s32[]{:S(2)}) async-start(), calls=%async_computation.6 | async-start | bytes 2359296 | tf_op jit(solution)/shard_map/all_gather | solution.py:778
  581.6 41.5 %copy-start.23 = (f32[128,896]{1,0:T(8,128)S(1)}, f32[128,896]{1,0:T(8,128)}, u32[]{:S(2)}) copy-start(f32[128,896]{1,0:T(8,128)} %get-tuple-element.769) | copy-start | bytes 1376260
  581.6 41.5 %copy-start.37 = (f32[128]{0:T(128)S(1)}, f32[128]{0:T(128)}, u32[]{:S(2)}) copy-start(f32[128]{0:T(128)} %get-tuple-element.818) | copy-start | bytes 1540
  626.8 22.5 %copy-start.16 = (f32[1,466012]{1,0:T(1,128)S(1)}, f32[1,466012]{1,0:T(1,128)}, u32[]{:S(2)}) copy-start(f32[1,466012]{1,0:T(1,128)} %param.25) | copy-start | bytes 5592148
  626.8 22.5 %copy-start.17 = (f32[1,466012]{1,0:T(1,128)S(1)}, f32[1,466012]{1,0:T(1,128)}, u32[]{:S(2)}) copy-start(f32[1,466012]{1,0:T(1,128)} %param.26) | copy-start | bytes 5592148
  (25 other events, 78.1 us)
Sparse Core Ops, SparseCore 0:
  205.6 94.3 all-gather.4
  480.2 35.6 reduce-scatter.1
  576.0 24.9 all-gather.6

commit v3 on v2

--- a/solution.py
+++ b/solution.py
@@ -135,6 +135,7 @@
 
 
 LANES = 128
+MESH = pl.DeviceIdType.MESH
 COLUMN_TILES = D // LANES
 VMEM_BYTES = 56 * 1024 * 1024
 MATRIX_COLS = QW + 2 * KEY_FEATURES + D
@@ -167,10 +168,58 @@
     ]
 
 
-def unpack_kernel(parts, flat_ref, attn_ref, wg_ref, wu_ref, wd_ref, vector_ref, held):
+def remote(source, target, sent_sem, landed_sem, device):
+    return pltpu.make_async_remote_copy(
+        src_ref=source,
+        dst_ref=target,
+        send_sem=sent_sem,
+        recv_sem=landed_sem,
+        device_id=device,
+        device_id_type=MESH,
+    )
+
+
+def meet(partners):
+    barrier = pltpu.get_barrier_semaphore()
+    for partner in partners:
+        pl.semaphore_signal(barrier, inc=1, device_id=partner, device_id_type=MESH)
+    pl.semaphore_wait(barrier, len(partners))
+
+
+def unpack_kernel(
+    parts, flat_ref, all_ref, vectors_ref, wg_ref, wu_ref, wd_ref,
+    attn_ref, vector_ref, held, attn_sems, vector_sems, pair_sems, own_sems,
+):
     bounds = shard_bounds(parts)
+    me_ctx, me_wt = lax.axis_index("ctx"), lax.axis_index("wt")
+    core = lax.rem(me_ctx, 2)
+    sibling = me_ctx + 1 - 2 * core
+    peers = [lax.rem(me_wt + step, parts) for step in range(1, parts)]
+    half = MATRIX_COLS // 2
+    mine = pl.ds(pl.multiple_of(core * half, half), half)
+    theirs = pl.ds(pl.multiple_of((1 - core) * half, half), half)
+    meet([(me_ctx, peer) for peer in peers] + [(sibling, me_wt)])
+
+    def attn_copy(peer, slot):
+        return remote(
+            attn_ref.at[:, mine], all_ref.at[slot, :, mine],
+            attn_sems.at[0, peer], attn_sems.at[1, slot], (me_ctx, peer),
+        )
+
+    def vector_copy(peer, slot):
+        return remote(
+            vector_ref, vectors_ref.at[slot],
+            vector_sems.at[0, peer], vector_sems.at[1, slot], (me_ctx, peer),
+        )
+
+    def pair_copy(slot, columns):
+        return remote(
+            all_ref.at[slot, :, columns], all_ref.at[slot, :, columns],
+            pair_sems.at[0, slot], pair_sems.at[1, slot], (sibling, me_wt),
+        )
+
     for number, (first_row, last_row) in enumerate(vector_rows(parts)):
-        vector_ref[number, 0 : last_row - first_row, :] = flat_ref[first_row:last_row, :]
+        vector_ref[number] = flat_ref[first_row : first_row + 16, :].astype(jnp.bfloat16)
 
     def extract(base, rows, tiles, out_ref, column):
         step = chunk_rows(rows)
@@ -200,27 +249,219 @@
 
     for base, rows, tiles, column in big_pieces(parts):
         extract(base, rows, tiles, attn_ref, column)
+    for peer in peers:
+        vector_copy(peer, me_wt).start()
+        attn_copy(peer, me_wt).start()
+    own_attn = pltpu.make_async_copy(attn_ref, all_ref.at[me_wt], own_sems.at[0])
+    own_vector = pltpu.make_async_copy(vector_ref, vectors_ref.at[me_wt], own_sems.at[1])
+    own_attn.start()
+    own_vector.start()
     for number, out_ref in ((9, wg_ref), (10, wu_ref), (11, wd_ref)):
         extract(bounds[number], FF // parts, COLUMN_TILES, out_ref, 0)
+    for peer in peers:
+        attn_copy(peer, peer).wait_recv()
+        pair_copy(peer, mine).start()
+    for peer in peers:
+        vector_copy(peer, peer).wait_recv()
+        pair_copy(peer, theirs).wait_recv()
+    own_attn.wait()
+    own_vector.wait()
+    for peer in peers:
+        pair_copy(peer, mine).wait_send()
+        attn_copy(peer, me_wt).wait_send()
+        vector_copy(peer, me_wt).wait_send()
 
 
 def unpack_weights(flat_rows, parts):
     whole = pl.BlockSpec(memory_space=pltpu.VMEM)
-    ff_rows = FF // parts
+    anywhere = pl.BlockSpec(memory_space=pl.ANY)
+    ff_shape = jax.ShapeDtypeStruct((FF // parts, D), jnp.bfloat16)
     return pl.pallas_call(
         lambda *refs: unpack_kernel(parts, *refs),
         out_shape=(
-            jax.ShapeDtypeStruct((D // parts, MATRIX_COLS), jnp.bfloat16),
-            jax.ShapeDtypeStruct((ff_rows, D), jnp.bfloat16),
-            jax.ShapeDtypeStruct((ff_rows, D), jnp.bfloat16),
-            jax.ShapeDtypeStruct((ff_rows, D), jnp.bfloat16),
-            jax.ShapeDtypeStruct((5, 8, LANES), jnp.float32),
+            jax.ShapeDtypeStruct((parts, D // parts, MATRIX_COLS), jnp.bfloat16),
+            jax.ShapeDtypeStruct((parts, 5, 16, LANES), jnp.bfloat16),
+            ff_shape,
+            ff_shape,
+            ff_shape,
         ),
         in_specs=[whole],
-        out_specs=(whole,) * 5,
-        scratch_shapes=[pltpu.VMEM((32 * COLUMN_TILES, LANES), jnp.float32)],
-        compiler_params=pltpu.CompilerParams(vmem_limit_bytes=VMEM_BYTES),
+        out_specs=(anywhere, anywhere, whole, whole, whole),
+        scratch_shapes=[
+            pltpu.VMEM((D // parts, MATRIX_COLS), jnp.bfloat16),
+            pltpu.VMEM((5, 16, LANES), jnp.bfloat16),
+            pltpu.VMEM((32 * COLUMN_TILES, LANES), jnp.float32),
+            pltpu.SemaphoreType.DMA((2, parts)),
+            pltpu.SemaphoreType.DMA((2, parts)),
+            pltpu.SemaphoreType.DMA((2, parts)),
+            pltpu.SemaphoreType.DMA((2,)),
+        ],
+        compiler_params=pltpu.CompilerParams(
+            collective_id=2, has_side_effects=True, vmem_limit_bytes=VMEM_BYTES
+        ),
     )(flat_rows)
+
+
+def gather_kernel(n_wt, count, *refs):
+    sources, outs = refs[:count], refs[count : 2 * count]
+    sems, own_sems = refs[2 * count :]
+    me_ctx, me_wt = lax.axis_index("ctx"), lax.axis_index("wt")
+    peers = [lax.rem(me_wt + step, n_wt) for step in range(1, n_wt)]
+    meet([(me_ctx, peer) for peer in peers])
+
+    def block(number, peer, slot):
+        return remote(
+            sources[number], outs[number].at[slot],
+            sems.at[number, 0, peer], sems.at[number, 1, slot], (me_ctx, peer),
+        )
+
+    for peer in peers:
+        for number in range(count):
+            block(number, peer, me_wt).start()
+    own = [
+        pltpu.make_async_copy(sources[number], outs[number].at[me_wt], own_sems.at[number])
+        for number in range(count)
+    ]
+    for copy in own:
+        copy.start()
+    for copy in own:
+        copy.wait()
+    for number in range(count):
+        for peer in peers:
+            block(number, peer, peer).wait_recv()
+            block(number, peer, me_wt).wait_send()
+
+
+def gather_wt(arrays, n_wt, collective_id):
+    count = len(arrays)
+    anywhere = pl.BlockSpec(memory_space=pl.ANY)
+    gathered = pl.pallas_call(
+        lambda *refs: gather_kernel(n_wt, count, *refs),
+        out_shape=tuple(jax.ShapeDtypeStruct((n_wt,) + x.shape, x.dtype) for x in arrays),
+        in_specs=[anywhere] * count,
+        out_specs=(anywhere,) * count,
+        scratch_shapes=[
+            pltpu.SemaphoreType.DMA((count, 2, n_wt)),
+            pltpu.SemaphoreType.DMA((count,)),
+        ],
+        compiler_params=pltpu.CompilerParams(collective_id=collective_id, has_side_effects=True),
+    )(*arrays)
+    return [x.reshape((-1,) + x.shape[2:]) for x in gathered]
+
+
+def reduce_kernel(
+    n_ctx, n_wt, owners, attn_ref, vector_ref, attn_sum_ref, vector_sum_ref,
+    landed, partial, vector_landed, vector_partial, vector_terms,
+    attn_sems, vector_sems, sum_sems, total_sems,
+):
+    me_ctx, me_wt = lax.axis_index("ctx"), lax.axis_index("wt")
+    wt_peers = [lax.rem(me_wt + step, n_wt) for step in range(1, n_wt)]
+    ctx_peers = [lax.rem(me_ctx + step, n_ctx) for step in range(1, n_ctx)]
+    meet([(me_ctx, peer) for peer in wt_peers] + [(peer, me_wt) for peer in ctx_peers])
+
+    def attn_copy(peer, slot):
+        return remote(
+            attn_ref.at[peer], landed.at[slot],
+            attn_sems.at[0, peer], attn_sems.at[1, slot], (peer, me_wt),
+        )
+
+    def vector_copy(peer, slot):
+        return remote(
+            vector_ref, vector_landed.at[slot],
+            vector_sems.at[0, peer], vector_sems.at[1, slot], (me_ctx, peer),
+        )
+
+    def sum_copy(owner, slot):
+        return remote(
+            partial, attn_sum_ref.at[slot],
+            sum_sems.at[0, owner], sum_sems.at[1, slot], (owner, me_wt),
+        )
+
+    def total_copy(owner, slot):
+        return remote(
+            vector_partial, vector_terms.at[slot],
+            total_sems.at[0, owner], total_sems.at[1, slot], (owner, me_wt),
+        )
+
+    for peer in wt_peers:
+        vector_copy(peer, me_wt).start()
+    for peer in ctx_peers:
+        attn_copy(peer, me_ctx).start()
+    vectors = vector_ref[...]
+    for peer in wt_peers:
+        vector_copy(peer, peer).wait_recv()
+        vectors = vectors + vector_landed[peer]
+    vector_partial[...] = vectors
+    for owner in range(owners):
+
+        @pl.when(me_ctx != owner)
+        def _(owner=owner):
+            total_copy(owner, me_ctx).start()
+
+    total = attn_ref[me_ctx].astype(jnp.float32)
+    for peer in ctx_peers:
+        attn_copy(peer, peer).wait_recv()
+        total = total + landed[peer].astype(jnp.float32)
+    partial[...] = total
+    for owner in range(owners):
+
+        @pl.when(me_ctx != owner)
+        def _(owner=owner):
+            sum_copy(owner, me_ctx).start()
+
+    attn_sum_ref[me_ctx] = total
+    vector_sum_ref[...] = vectors
+
+    @pl.when(me_ctx < owners)
+    def _():
+        summed = vectors
+        for peer in ctx_peers:
+            total_copy(0, peer).wait_recv()
+            summed = summed + vector_terms[peer]
+        vector_sum_ref[...] = summed
+        for peer in ctx_peers:
+            sum_copy(0, peer).wait_recv()
+
+    for owner in range(owners):
+
+        @pl.when(me_ctx != owner)
+        def _(owner=owner):
+            total_copy(owner, me_ctx).wait_send()
+            sum_copy(owner, me_ctx).wait_send()
+
+    for peer in wt_peers:
+        vector_copy(peer, me_wt).wait_send()
+    for peer in ctx_peers:
+        attn_copy(peer, me_ctx).wait_send()
+
+
+def reduce_attention(attn_grads, vectors, n_wt, owners):
+    n_ctx = attn_grads.shape[0]
+    whole = pl.BlockSpec(memory_space=pltpu.VMEM)
+    block = attn_grads.shape[1:]
+    return pl.pallas_call(
+        lambda *refs: reduce_kernel(n_ctx, n_wt, owners, *refs),
+        out_shape=(
+            jax.ShapeDtypeStruct(attn_grads.shape, jnp.float32),
+            jax.ShapeDtypeStruct(vectors.shape, jnp.float32),
+        ),
+        in_specs=[whole] * 2,
+        out_specs=(whole, whole),
+        scratch_shapes=[
+            pltpu.VMEM(attn_grads.shape, jnp.bfloat16),
+            pltpu.VMEM(block, jnp.float32),
+            pltpu.VMEM((n_wt,) + vectors.shape, jnp.float32),
+            pltpu.VMEM(vectors.shape, jnp.float32),
+            pltpu.VMEM((n_ctx,) + vectors.shape, jnp.float32),
+            pltpu.SemaphoreType.DMA((2, n_ctx)),
+            pltpu.SemaphoreType.DMA((2, n_wt)),
+            pltpu.SemaphoreType.DMA((2, n_ctx)),
+            pltpu.SemaphoreType.DMA((2, n_ctx)),
+        ],
+        compiler_params=pltpu.CompilerParams(
+            collective_id=3, has_side_effects=True, vmem_limit_bytes=VMEM_BYTES
+        ),
+    )(attn_grads, vectors)
 
 
 def small_rows(vectors, bases):
@@ -246,8 +487,8 @@
 
 
 def assemble_kernel(
-    parts, row_of_small, place_ref, small_ref, attn_ref, terms_ref, own_ref, grad_ref, param_ref,
-    flat, held,
+    parts, row_of_small, place_ref, small_ref, attn_ref, terms_ref, own_ref, first_ref, second_ref,
+    grad_ref, param_ref, new_first_ref, new_second_ref, flat, held,
 ):
     senders, taken = terms_ref.shape[0], terms_ref.shape[1]
     prefix = shard_bounds(parts)[9]
@@ -302,44 +543,56 @@
         insert(base, rows, tiles, from_attn(column))
     insert(prefix, taken, COLUMN_TILES, from_terms)
 
-    def shift(source, row_start, lane, out_ref):
+    def shifted(source, row_start, lane, at, step):
+        turn = (LANES - lane) % LANES
+        low = pltpu.roll(source[pl.ds(row_start + at, step), :], turn, 1)
+        high = pltpu.roll(source[pl.ds(row_start + at + 1, step), :], turn, 1)
+        return jnp.where(lane_ids(step) < LANES - lane, low, high)
+
+    def update(number, carry):
         step = 64
-        turn = (LANES - lane) % LANES
-
-        def chunk(number, carry):
-            at = row_start + number * step
-            low = pltpu.roll(source[pl.ds(at, step), :], turn, 1)
-            high = pltpu.roll(source[pl.ds(at + 1, step), :], turn, 1)
-            out_ref[pl.ds(pl.multiple_of(number * step, step), step), :] = jnp.where(
-                lane_ids(step) < LANES - lane, low, high
-            )
-            return carry
-
-        lax.fori_loop(0, out_rows // step, chunk, 0)
-
-    shift(flat, place_ref[0], place_ref[1], grad_ref)
-    shift(own_ref, place_ref[2], place_ref[3], param_ref)
-
-
-def assemble(parts, small, row_of_small, attn_sum, terms, own_rows, place, out_rows):
+        at = number * step
+        rows = pl.ds(pl.multiple_of(at, step), step)
+        grad = shifted(flat, place_ref[0], place_ref[1], at, step)
+        own = shifted(own_ref, place_ref[2], place_ref[3], at, step)
+        index_vec = (
+            place_ref[4]
+            + (lax.broadcasted_iota(jnp.int32, (step, LANES), 0) + at) * LANES
+            + lane_ids(step)
+        )
+        decay = decay_mask(index_vec, parts)
+        first = beta_one * first_ref[rows, :] + (1.0 - beta_one) * grad
+        second = beta_two * second_ref[rows, :] + (1.0 - beta_two) * grad * grad
+        m_hat = first / (1.0 - beta_one**step_count)
+        v_hat = second / (1.0 - beta_two**step_count)
+        grad_ref[rows, :] = grad
+        new_first_ref[rows, :] = first
+        new_second_ref[rows, :] = second
+        param_ref[rows, :] = own - learn_rate * (
+            m_hat / (jnp.sqrt(v_hat) + adam_eps) + decay_rate * decay * own
+        )
+        return carry
+
+    lax.fori_loop(0, out_rows // 64, update, 0)
+
+
+def assemble(parts, small, row_of_small, attn_sum, terms, own_rows, first, second, place):
+    out_rows = first.shape[0]
     whole = pl.BlockSpec(memory_space=pltpu.VMEM)
     prefix = shard_bounds(parts)[9]
     flat_rows = prefix // LANES + terms.shape[1] * COLUMN_TILES + out_rows // 8 * 8 + 80
     shape = jax.ShapeDtypeStruct((out_rows, LANES), jnp.float32)
     return pl.pallas_call(
         lambda *refs: assemble_kernel(parts, row_of_small, *refs),
-        out_shape=(shape, shape),
-        in_specs=[pl.BlockSpec(memory_space=pltpu.SMEM)] + [whole] * 4,
-        out_specs=(whole, whole),
+        out_shape=(shape,) * 4,
+        in_specs=[pl.BlockSpec(memory_space=pltpu.SMEM)] + [whole] * 6,
+        out_specs=(whole,) * 4,
         scratch_shapes=[
             pltpu.VMEM((flat_rows, LANES), jnp.float32),
             pltpu.VMEM((16 * COLUMN_TILES, LANES), jnp.float32),
         ],
         compiler_params=pltpu.CompilerParams(vmem_limit_bytes=VMEM_BYTES),
-    )(place, small, attn_sum, terms, own_rows)
-
-
-MESH = pl.DeviceIdType.MESH
+    )(place, small, attn_sum, terms, own_rows, first, second)
 
 
 def exchange_kernel(
@@ -476,12 +729,10 @@
     bounds = shard_bounds(n_wt)
     prefix = bounds[9]
     shard_len = params.shape[1]
-    flat_params = jnp.pad(params[0], (0, -shard_len % 1024 + 10240)).reshape(-1, LANES)
-    attn_own, wg_own, wu_own, wd_own, vector_held = unpack_weights(flat_params, n_wt)
+    flat_params = jnp.pad(params, ((0, 0), (0, -shard_len % 1024 + 10240))).reshape(-1, LANES)
+    attn_all, vectors_all, wg_own, wu_own, wd_own = unpack_weights(flat_params, n_wt)
+    attn_all = attn_all.reshape(D, MATRIX_COLS)
     vector_numbers = (0, 2, 4, 6, 8)
-    vectors_own = vector_held.astype(jnp.bfloat16)
-    attn_all = lax.all_gather(attn_own, "wt", axis=0, tiled=True)
-    vectors_all = lax.all_gather(vectors_own, "wt", axis=0)
     wq_b = attn_all[:, :QW]
     wk_b = attn_all[:, QW : QW + KEY_FEATURES]
     wv_b = attn_all[:, QW + KEY_FEATURES : QW + 2 * KEY_FEATURES]
@@ -491,7 +742,7 @@
         lane = bounds[number] % LANES
         width = bounds[number + 1] - bounds[number]
         vector_parts.append(
-            vectors_all[:, place_no].reshape(n_wt, 8 * LANES)[:, lane : lane + width].reshape(-1)
+            vectors_all[:, place_no].reshape(n_wt, 16 * LANES)[:, lane : lane + width].reshape(-1)
         )
     gain_b, bq_b, bk_b, bv_b, gain_two = vector_parts
     gain_full = gain_b.astype(jnp.float32)
@@ -752,44 +1003,36 @@
         d_scaled * x_rows, -1, keepdims=True
     )
     input_grad = d_mid + d_input
-    mid_group, query_grads, key_grads_group, value_grads_group = (
-        lax.all_gather(d_mid_bf, "wt", axis=0, tiled=True),
-        lax.all_gather(dq_bf, "wt", axis=0, tiled=True),
-        lax.all_gather(dk_bf, "wt", axis=0, tiled=True),
-        lax.all_gather(dv_bf, "wt", axis=0, tiled=True),
+    mid_group, query_grads, key_value_grads = gather_wt(
+        [d_mid_bf, dq_bf, jnp.concatenate([dk_bf, dv_bf], 1)], n_wt, 4
     )
     attn_grads = jnp.concatenate(
         [
             outer_dot(feature_cols, query_grads),
-            outer_dot(feature_cols, key_grads_group),
-            outer_dot(feature_cols, value_grads_group),
+            outer_dot(feature_cols, key_value_grads),
             outer_dot(context_cols, mid_group),
         ],
         1,
     ).astype(jnp.bfloat16)
     attn_part = attn_grads.shape[0] // n_ctx
-    attn_terms = lax.all_to_all(
+    vectors = jnp.concatenate(
+        [
+            grad_gain,
+            jnp.sum(dq_bf.astype(jnp.float32), 0),
+            jnp.sum(dk_bf.astype(jnp.float32), 0),
+            jnp.sum(dv_bf.astype(jnp.float32), 0),
+            grad_gain_two,
+        ]
+    )
+    vectors = jnp.pad(vectors, (0, -vectors.shape[0] % 1024)).reshape(-1, LANES)
+    attn_sum, vector_sums = reduce_attention(
         attn_grads.reshape(n_ctx, attn_part, MATRIX_COLS),
-        "ctx",
-        split_axis=0,
-        concat_axis=0,
-        tiled=True,
-    )
-    attn_sum = lax.all_gather(
-        jnp.sum(attn_terms.astype(jnp.float32), 0), "ctx", axis=0, tiled=True
-    )
-    vector_sums = lax.psum(
-        jnp.concatenate(
-            [
-                grad_gain,
-                jnp.sum(dq_bf.astype(jnp.float32), 0),
-                jnp.sum(dk_bf.astype(jnp.float32), 0),
-                jnp.sum(dv_bf.astype(jnp.float32), 0),
-                grad_gain_two,
-            ]
-        ),
-        ("ctx", "wt"),
-    )
+        vectors,
+        n_wt,
+        -(-prefix // piece_len),
+    )
+    attn_sum = attn_sum.reshape(n_ctx * attn_part, MATRIX_COLS)
+    vector_sums = vector_sums.reshape(-1)
     small = []
     left = 0
     for full in (D, QW, KEY_FEATURES, KEY_FEATURES, D):
@@ -809,23 +1052,24 @@
             flat_start % LANES,
             piece_start // LANES - own_row,
             piece_start % LANES,
+            piece_start,
         ]
     ).astype(jnp.int32)
-    grad_rows, param_rows = assemble(
-        n_wt, small, row_of_small, attn_sum, ff_terms, own_rows, place, out_rows
-    )
-    param_grad = grad_rows.reshape(1, -1)[:, :piece_len]
-    own_params = param_rows.reshape(1, -1)[:, :piece_len]
-    decay = decay_mask(piece_start + jnp.arange(piece_len, dtype=jnp.int32), n_wt).reshape(
-        1, piece_len
-    )
-    new_moment1 = beta_one * moment1 + (1.0 - beta_one) * param_grad
-    new_moment2 = beta_two * moment2 + (1.0 - beta_two) * param_grad * param_grad
-    m_hat = new_moment1 / (1.0 - beta_one**step_count)
-    v_hat = new_moment2 / (1.0 - beta_two**step_count)
-    new_params = own_params - learn_rate * (
-        m_hat / (jnp.sqrt(v_hat) + adam_eps) + decay_rate * decay * own_params
-    )
+    tail = ((0, 0), (0, out_rows * LANES - piece_len))
+    updated = assemble(
+        n_wt,
+        small,
+        row_of_small,
+        attn_sum,
+        ff_terms,
+        own_rows,
+        jnp.pad(moment1, tail).reshape(out_rows, LANES),
+        jnp.pad(moment2, tail).reshape(out_rows, LANES),
+        place,
+    )
+    param_grad, new_params, new_moment1, new_moment2 = [
+        rows.reshape(1, -1)[:, :piece_len] for rows in updated
+    ]
     return (
         block_out.reshape(1, token_rows, D),
         input_grad.reshape(1, token_rows, D),

time: 693 us -> 464 us (0.67)
  other arithmetic: 214 us -> 22.2 us
  blocking collectives: 182 us -> 52.1 us
  Pallas kernels: 105 us -> 196 us
  local copies, waits for them, and re-layouts: 46.8 us -> 80.7 us
  waiting for transfers between devices: 44.6 us -> 17.9 us
  matrix products: 53.8 us -> 46.4 us
    unnamed x4 -> x3, other arithmetic: 163 us -> 2.04 us
    all_gather x5 -> x0, blocking collectives: 79 us -> none  [the longest x1 20 us: body(): lax.all_gather(d_mid_bf, 'wt', axis=0, tiled=True)]
    pallas_call x0 -> x2, Pallas kernels: none -> 68.7 us  [the longest x1 38.6 us: gather_wt(): pl.pallas_call(lambda *refs: gather_kernel(n_wt, count, *refs), out_shape...]
    psum x1 -> x0, blocking collectives: 38.1 us -> none  [body(): lax.psum(jnp.concatenate([grad_gain, jnp.sum(dq_bf.astype(jnp.float32), 0...]
    sub x1 -> x0, other arithmetic: 31.4 us -> none  [body(): own_params - learn_rate * (m_hat / (jnp.sqrt(v_hat) + adam_eps) + decay_r...]
    all_gather x2 -> x0, waiting for transfers between devices: 30.9 us -> none  [the longest x1 30.9 us: body(): attn_all = lax.all_gather(attn_own, 'wt', axis=0, tiled=True)]
    pad x0 -> x3, local copies, waits for them, and re-layouts: none -> 30.2 us  [the longest x1 23.4 us: body(): jnp.pad(params, ((0, 0), (0, -shard_len % 1024 + 10240))).reshape(-1, LANES)]
    pallas_call x1, Pallas kernels: 26.5 us -> 50.4 us  [unpack_weights(): pl.pallas_call(lambda *refs: unpack_kernel(parts, *refs), out_shape=(jax....]
  transfers between devices with their start and end apart: 6 -> 3, of which waited for: 2 -> 2; matrix products, arithmetic and copies ran while one was open for 9% -> 22% of each run, Pallas kernels for 8% -> 20%
where the time goes in v3:
time: 464 us; the launch traced here: 463 us
  Pallas kernels  196 us (42%)
  local copies, waits for them, and re-layouts  80.7 us (17%)
  blocking collectives  52.1 us (11%)
  matrix products  46.4 us (10%)
  starting transfers between devices  28.3 us (6%)
  other arithmetic  22.2 us (5%)
  between operations  18.6 us (4%)
  waiting for transfers between devices  17.9 us (4%)
    pallas_call x1, Pallas kernels, exchange(): pl.pallas_call(lambda *refs: exchange_kernel(n_ctx, n_wt, *refs), out_sha...  55 us
    pallas_call x1, Pallas kernels, unpack_weights(): pl.pallas_call(lambda *refs: unpack_kernel(parts, *refs), out_shape=(jax....  50.4 us
    pallas_call x1, Pallas kernels, gather_wt(): pl.pallas_call(lambda *refs: gather_kernel(n_wt, count, *refs), out_shape...  38.6 us
    pallas_call x1, Pallas kernels, reduce_attention(): pl.pallas_call(lambda *refs: reduce_kernel(n_ctx, n_wt, owners, *refs), o...  30.1 us
    pad x1, local copies, waits for them, and re-layouts, body(): jnp.pad(params, ((0, 0), (0, -shard_len % 1024 + 10240))).reshape(-1, LANES)  23.4 us
    all_gather x1, blocking collectives, body(): lax.all_gather(cot_bf, 'wt', axis=0, tiled=True)  22 us
    pallas_call x1, Pallas kernels, assemble(): pl.pallas_call(lambda *refs: assemble_kernel(parts, row_of_small, *refs),...  21.6 us
    all_gather x1, blocking collectives, body(): lax.all_gather(normed_two, 'wt', axis=0, tiled=True)  20 us
  transfers between devices with their start and end apart: 3, of which 2 were waited for; matrix products, arithmetic and copies ran while one was open for 22% of the time, Pallas kernels for 20%

profile of v3, /device:TPU:0, one launch (start us, length us, event | category | flops | bytes accessed | tf_op | source)
XLA Modules:
  0.0 462.5 jit_solution(2485559614077879039)
XLA Ops:
  10.0 23.4 %pad.38 = f32[1,3738624]{1,0:T(1,128)} pad(f32[1,3728096]{1,0:T(1,128)} %param.24, f32[]{:T(128)} %constant.273.clone.1), padding=0_0x0_10528 | pad | bytes 29866884 | tf_op jit(solution)/shard_map/jit(_pad)/pad | solution.py:732
  33.4 50.4 %shard_map.127 = (bf16[4,224,2048]{2,1,0:T(8,128)(2,1)}, bf16[4,5,16,128]{3,2,1,0:T(8,128)(2,1)}, bf16[1216,896]{1,0:T(8,128)(2,1)}, bf16[1216,896]{1,0:T(8,128)(2,1)}, bf16[1216,896]{1,0:T(8,128)(2,1)}) custom-call(f32[29208,128]{1,0:T(8,128)} %bitcast.510), custom_call_target="tpu_custom_call" | custom-call | tf_op jit(solution)/shard_map/pallas_call | solution.py:279
  85.6 13.4 %all-to-all-start = ((bf16[128,4,224]{0,2,1:T(8,128)(2,1)}), bf16[128,4,224]{0,2,1:T(8,128)(2,1)}, u32[]{:S(2)}, u32[]{:S(2)}) async-start(bf16[128,4,224]{0,2,1:T(8,128)(2,1)} %multiply_convert_fusion.3), calls=%async_computation.1 | async-start | bytes 458752 | tf_op jit(solution)/shard_map/all_to_all | solution.py:854
  102.8 22.0 %all_gather.11 = bf16[512,896]{1,0:T(8,128)(2,1)} all-gather(bf16[128,896]{1,0:T(8,128)(2,1)S(1)} %bitcast_convert_fusion), channel_id=1, replica_groups=mesh['ctx'=8,'wt'=4] {'wt'}, dimensions={0}, use_global_device_ids=true | all-gather | bytes 1146880 | tf_op jit(solution)/shard_map/all_gather | solution.py:864
  130.3 10.0 %all_gather.9 = bf16[1024,256]{0,1:T(8,128)(2,1)S(1)} all-gather(bf16[128,256]{0,1:T(8,128)(2,1)S(1)} %pad_maximum_fusion.6), channel_id=1, replica_groups=mesh['ctx'=8,'wt'=4] {'ctx'}, dimensions={0}, use_global_device_ids=true | all-gather | bytes 589824 | tf_op jit(solution)/shard_map/all_gather | solution.py:767
  140.5 3.9 gather_fusion
  156.6 20.0 %all_gather.10 = bf16[512,896]{1,0:T(8,128)(2,1)S(1)} all-gather(bf16[128,896]{1,0:T(8,128)(2,1)S(1)} %multiply_convert_fusion.4), channel_id=1, replica_groups=mesh['ctx'=8,'wt'=4] {'wt'}, dimensions={0}, use_global_device_ids=true | all-gather | bytes 1146880 | tf_op jit(solution)/shard_map/all_gather | solution.py:863
  185.6 2.8 fusion.152
  192.5 2.8 convolution_add_fusion
  203.6 55.0 %shard_map.128 = (f32[128,896]{1,0:T(8,128)}, f32[128,896]{1,0:T(8,128)}, bf16[4,544,896]{2,1,0:T(8,128)(2,1)}) custom-call(f32[4,128,896]{2,1,0:T(8,128)} %bitcast.540, f32[4,128,896]{2,1,0:T(8,128)} %bitcast.560, bf16[8,544,896]{2,1,0:T(8,128)(2,1)} %fusion.83.refs_2_), custom_call_target="tpu_custom_call" | custom-call | tf_op jit(solution)/shard_map/pallas_call | solution.py:701
  265.1 4.0 while.78
  269.1 8.0 %while.79 = (s32[]{:T(128)}, f32[64,2,7,64]{0,3,2,1:T(8,128)S(1)}, f32[1024,256]{0,1:T(8,128)S(1)}, s32[]{:T(128)}, bf16[1024,256]{0,1:T(8,128)(2,1)S(1)}, /*ind...) while((s32[]{:T(128)}, f32[64,2,7,64]{0,3,2,1:T(8,128)S(1)}, ...), condition=%wide.region_23.24_spmd.clone, body=%wide.region_22.23_spmd.clone.sunk | while | flops 297747008 | bytes 12726007 | solution.py:960
  277.8 3.5 gather_fusion.1
  291.3 3.4 pad.46
  294.7 3.4 pad.47
  299.7 3.0 constant_dynamic-slice_fusion.6.refs_4_
  302.7 15.3 %reduce-scatter.2.cloned.1.call-done = f32[128,256]{1,0:T(8,128)} async-done(((f32[1024,256]{1,0:T(8,128)}), f32[128,256]{1,0:T(8,128)}) %reduce-scatter.2.cloned.1.call-update) | async-done | bytes 131088 | tf_op jit(solution)/shard_map/reduce_scatter | solution.py:989
  325.2 38.6 %shard_map.129 = (bf16[4,128,896]{2,1,0:T(8,128)(2,1)}, bf16[4,128,896]{2,1,0:T(8,128)(2,1)}, bf16[4,128,256]{2,1,0:T(8,128)(2,1)}) custom-call(bf16[128,896]{1,0:T(8,128)(2,1)} %copy-done.11, bf16[128,896]{1,0:T(8,128)(2,1)} %copy-done.12, bf16[128,256]{1,0:T(8,128)(2,1)} %pad_maximum_fusion.8.refs_2_), custom_call_target="tpu_custom_call" | custom-call | tf_op jit(solution)/shard_map/pallas_call | solution.py:338
  363.9 14.9 %all-to-all-start.1 = ((bf16[128,4,224]{0,2,1:T(8,128)(2,1)}), bf16[128,4,224]{0,2,1:T(8,128)(2,1)S(1)}, u32[]{:S(2)}, u32[]{:S(2)}) async-start(bf16[128,4,224]{0,2,1:T(8,128)(2,1)} %pad_maximum_fusion.5), calls=%async_computation.2 | async-start | bytes 458752 | tf_op jit(solution)/shard_map/all_to_all | solution.py:855
  383.0 2.6 all-to-all-done.1
  388.1 30.1 %shard_map.130 = (f32[8,28,2048]{2,1,0:T(8,128)}, f32[24,128]{1,0:T(8,128)}) custom-call(bf16[8,28,2048]{2,1,0:T(8,128)(2,1)} %pad_maximum_fusion.refs_0_, f32[24,128]{1,0:T(8,128)} %pad_bitcast_fusion.refs_1_), custom_call_target="tpu_custom_call" | custom-call | tf_op jit(solution)/shard_map/pallas_call | solution.py:442
  420.2 2.8 reshape.544.refs_2_
  423.7 21.6 %shard_map.131 = (f32[3648,128]{1,0:T(8,128)}, f32[3648,128]{1,0:T(8,128)}, f32[3648,128]{1,0:T(8,128)}, f32[3648,128]{1,0:T(8,128)}) custom-call(s32[5]{0:T(128)} %stack.56.refs_0_, f32[16,128]{1,0:T(8,128)} %pad.45.refs_1_, f32[224,2048]{1,0:T(8,128)} %reshape.544.refs_2_, bf16[4,544,896]{2,1,0:T(8,128)(2,1)} %get-tuple-element.307.refs_3_, ...), custom_call_target="tpu_custom_call" | custom-call | tf_op jit(solution)/shard_map/pallas_call | solution.py:585
  445.2 3.8 slice.246
  (330 shorter events, 103.1 us)
Async XLA Ops:
  10.0 115.4 %copy-start.36 = (f32[128]{0:T(128)}, f32[128]{0:T(128)S(1)}, u32[]{:S(2)}) copy-start(f32[128]{0:T(128)S(1)} %get-tuple-element.733) | copy-start | bytes 1540
  33.4 65.6 %copy-start.39 = (s32[8]{0:T(128)S(1)}, s32[8]{0:T(128)}, u32[]{:S(2)}) copy-start(s32[8]{0:T(128)} %param.22) | copy-start | bytes 100
  33.4 65.6 %copy-start.41 = (s32[8]{0:T(128)S(1)}, s32[8]{0:T(128)}, u32[]{:S(2)}) copy-start(s32[8]{0:T(128)} %constant.313.clone) | copy-start | bytes 100
  33.4 68.4 %copy-start.44 = (s32[1,128]{1,0:T(1,128)S(1)}, s32[1,128]{1,0:T(1,128)}, u32[]{:S(2)}) copy-start(s32[1,128]{1,0:T(1,128)} %param.23) | copy-start | bytes 1540
  33.4 69.3 %copy-start.21 = (f32[1,128,896]{2,1,0:T(8,128)S(1)}, f32[1,128,896]{2,1,0:T(8,128)}, u32[]{:S(2)}) copy-start(f32[1,128,896]{2,1,0:T(8,128)} %param.21) | copy-start | bytes 1376260
  83.8 41.6 %copy-start = (f32[1,128,896]{2,1,0:T(8,128)S(1)}, f32[1,128,896]{2,1,0:T(8,128)}, u32[]{:S(2)}) copy-start(f32[1,128,896]{2,1,0:T(8,128)} %param.20) | copy-start | bytes 1376260
  85.6 278.2 %all-to-all-start = ((bf16[128,4,224]{0,2,1:T(8,128)(2,1)}), bf16[128,4,224]{0,2,1:T(8,128)(2,1)}, u32[]{:S(2)}, u32[]{:S(2)}) async-start(bf16[128,4,224]{0,2,1:T(8,128)(2,1)} %multiply_convert_fusion.3), calls=%async_computation.1 | async-start | bytes 458752 | tf_op jit(solution)/shard_map/all_to_all | solution.py:854
  99.0 219.0 %reduce-scatter.2.cloned.1.call-start = ((), (), s32[]{:S(2)}) async-start(), calls=%async_computation.3 | async-start | bytes 1179648 | tf_op jit(solution)/shard_map/reduce_scatter | solution.py:989
  148.1 5.7 %copy-start.5 = (f32[2,7,64,64]{3,2,1,0:T(8,128)}, f32[2,7,64,64]{3,2,1,0:T(8,128)S(1)}, u32[]{:S(2)}) copy-start(f32[2,7,64,64]{3,2,1,0:T(8,128)S(1)} %get-tuple-element.289) | copy-start | bytes 688132
  154.4 22.3 %copy-start.43 = (bf16[1216,896]{1,0:T(8,128)(2,1)S(1)}, bf16[1216,896]{1,0:T(8,128)(2,1)}, u32[]{:S(2)}) copy-start(bf16[1216,896]{1,0:T(8,128)(2,1)} %get-tuple-element.294) | copy-start | bytes 6537220
  203.6 56.2 %copy-start.22 = (f32[1,128,896]{2,1,0:T(8,128)S(1)}, f32[1,128,896]{2,1,0:T(8,128)}, u32[]{:S(2)}) copy-start(f32[1,128,896]{2,1,0:T(8,128)} %param.21) | copy-start | bytes 1376260
  265.1 4.1 copy-start.35
  287.4 3.9 copy-start.13
  294.7 4.1 copy-start.26
  294.7 4.1 copy-start.27
  294.7 4.9 %copy-start.18 = (f32[128,896]{1,0:T(8,128)S(1)}, f32[128,896]{1,0:T(8,128)}, u32[]{:S(2)}) copy-start(f32[128,896]{1,0:T(8,128)} %copy.101) | copy-start | bytes 1376260
  294.7 4.9 %copy-start.19 = (f32[128,896]{1,0:T(8,128)S(1)}, f32[128,896]{1,0:T(8,128)}, u32[]{:S(2)}) copy-start(f32[128,896]{1,0:T(8,128)} %copy.102) | copy-start | bytes 1376260
  294.7 4.9 %copy-start.20 = (f32[128,896]{1,0:T(8,128)S(1)}, f32[128,896]{1,0:T(8,128)}, u32[]{:S(2)}) copy-start(f32[128,896]{1,0:T(8,128)} %copy.100) | copy-start | bytes 1376260
  299.7 23.3 %copy-start.12 = (bf16[128,896]{1,0:T(8,128)(2,1)}, bf16[128,896]{1,0:T(8,128)(2,1)S(1)}, u32[]{:S(2)}) copy-start(bf16[128,896]{1,0:T(8,128)(2,1)S(1)} %add_convert_fusion.refs_1_) | copy-start | bytes 688132
  299.7 19.4 %copy-start.29 = (f32[128,128]{1,0:T(8,128)S(1)}, f32[128,128]{1,0:T(8,128)}, u32[]{:S(2)}) copy-start(f32[128,128]{1,0:T(8,128)} %copy.104) | copy-start | bytes 196612
  302.7 20.3 %copy-start.37 = (f32[128]{0:T(128)S(1)}, f32[128]{0:T(128)}, u32[]{:S(2)}) copy-start(f32[128]{0:T(128)} %copy-done.36) | copy-start | bytes 1540
  363.8 16.7 %copy-start.28 = (bf16[4,128,256]{2,1,0:T(8,128)(2,1)S(1)}, bf16[4,128,256]{2,1,0:T(8,128)(2,1)}, u32[]{:S(2)}) copy-start(bf16[4,128,256]{2,1,0:T(8,128)(2,1)} %get-tuple-element.303) | copy-start | bytes 786436
  363.8 21.8 %copy-start.25 = (bf16[4,128,896]{2,1,0:T(8,128)(2,1)S(1)}, bf16[4,128,896]{2,1,0:T(8,128)(2,1)}, u32[]{:S(2)}) copy-start(bf16[4,128,896]{2,1,0:T(8,128)(2,1)} %get-tuple-element.304) | copy-start | bytes 2752516
  363.9 21.7 %all-to-all-start.1 = ((bf16[128,4,224]{0,2,1:T(8,128)(2,1)}), bf16[128,4,224]{0,2,1:T(8,128)(2,1)S(1)}, u32[]{:S(2)}, u32[]{:S(2)}) async-start(bf16[128,4,224]{0,2,1:T(8,128)(2,1)} %pad_maximum_fusion.5), calls=%async_computation.2 | async-start | bytes 458752 | tf_op jit(solution)/shard_map/all_to_all | solution.py:855
  (25 other events, 43.9 us)
Sparse Core Ops, SparseCore 0:
  282.6 35.3 reduce-scatter.1

commit v4 on v3

--- a/solution.py
+++ b/solution.py
@@ -302,16 +302,19 @@
     )(flat_rows)
 
 
-def gather_kernel(n_wt, count, *refs):
+def gather_kernel(n_wt, count, scattered, *refs):
     sources, outs = refs[:count], refs[count : 2 * count]
     sems, own_sems = refs[2 * count :]
     me_ctx, me_wt = lax.axis_index("ctx"), lax.axis_index("wt")
     peers = [lax.rem(me_wt + step, n_wt) for step in range(1, n_wt)]
     meet([(me_ctx, peer) for peer in peers])
 
+    def part(number, peer):
+        return sources[number].at[peer] if number < scattered else sources[number]
+
     def block(number, peer, slot):
         return remote(
-            sources[number], outs[number].at[slot],
+            part(number, peer), outs[number].at[slot],
             sems.at[number, 0, peer], sems.at[number, 1, slot], (me_ctx, peer),
         )
 
@@ -319,7 +322,7 @@
         for number in range(count):
             block(number, peer, me_wt).start()
     own = [
-        pltpu.make_async_copy(sources[number], outs[number].at[me_wt], own_sems.at[number])
+        pltpu.make_async_copy(part(number, me_wt), outs[number].at[me_wt], own_sems.at[number])
         for number in range(count)
     ]
     for copy in own:
@@ -332,12 +335,15 @@
             block(number, peer, me_wt).wait_send()
 
 
-def gather_wt(arrays, n_wt, collective_id):
+def gather_wt(arrays, n_wt, scattered, collective_id):
     count = len(arrays)
+    blocks = [x.shape[1:] if k < scattered else x.shape for k, x in enumerate(arrays)]
     anywhere = pl.BlockSpec(memory_space=pl.ANY)
     gathered = pl.pallas_call(
-        lambda *refs: gather_kernel(n_wt, count, *refs),
-        out_shape=tuple(jax.ShapeDtypeStruct((n_wt,) + x.shape, x.dtype) for x in arrays),
+        lambda *refs: gather_kernel(n_wt, count, scattered, *refs),
+        out_shape=tuple(
+            jax.ShapeDtypeStruct((n_wt,) + block, x.dtype) for block, x in zip(blocks, arrays)
+        ),
         in_specs=[anywhere] * count,
         out_specs=(anywhere,) * count,
         scratch_shapes=[
@@ -850,10 +856,10 @@
     ctx_late, lse_late = attend(query_flat[half_rows:], late_block)
     context_rows = jnp.concatenate([ctx_early, ctx_late], 0)
     context_bf = context_rows.astype(jnp.bfloat16)
-    feature_cols, context_cols = (
-        lax.all_to_all(normed, "wt", split_axis=1, concat_axis=0, tiled=True),
-        lax.all_to_all(context_bf, "wt", split_axis=1, concat_axis=0, tiled=True),
-    )
+
+    def by_feature_shard(rows):
+        return jnp.transpose(rows.reshape(token_rows, n_wt, D // n_wt), (1, 0, 2))
+
     mid_rows = x_rows + jnp.dot(context_bf, wo_b, preferred_element_type=jnp.float32)
     gain_two_full = gain_two.astype(jnp.float32)
     inv_rms_two = lax.rsqrt(jnp.mean(mid_rows * mid_rows, -1, keepdims=True) + norm_eps)
@@ -1003,8 +1009,17 @@
         d_scaled * x_rows, -1, keepdims=True
     )
     input_grad = d_mid + d_input
-    mid_group, query_grads, key_value_grads = gather_wt(
-        [d_mid_bf, dq_bf, jnp.concatenate([dk_bf, dv_bf], 1)], n_wt, 4
+    feature_cols, context_cols, mid_group, query_grads, key_value_grads = gather_wt(
+        [
+            by_feature_shard(normed),
+            by_feature_shard(context_bf),
+            d_mid_bf,
+            dq_bf,
+            jnp.concatenate([dk_bf, dv_bf], 1),
+        ],
+        n_wt,
+        2,
+        4,
     )
     attn_grads = jnp.concatenate(
         [

time: 464 us -> 464 us (level)
  starting transfers between devices: 28.3 us -> 0.04 us
  Pallas kernels: 196 us -> 215 us
  blocking collectives: 52.1 us -> 62.2 us
  waiting for transfers between devices: 17.9 us -> 9.2 us
  other arithmetic: 22.2 us -> 27.3 us
    all_to_all x2 -> x0, starting transfers between devices: 28.3 us -> none  [the longest x1 14.9 us: body(): lax.all_to_all(context_bf, 'wt', split_axis=1, concat_axis=0, tiled=True)]
    pallas_call x1, Pallas kernels: 30.1 us -> 43.8 us  [reduce_attention(): pl.pallas_call(lambda *refs: reduce_kernel(n_ctx, n_wt, owners, *refs), o...]
    all_gather x1, blocking collectives: 20 us -> 29 us  [body(): lax.all_gather(normed_two, 'wt', axis=0, tiled=True)]
    pallas_call x1, Pallas kernels: 38.6 us -> 47.2 us  [gather_wt(): pl.pallas_call(lambda *refs: gather_kernel(n_wt, count, scattered, *refs)...]
    reduce_scatter x1, waiting for transfers between devices: 15.3 us -> 9.18 us  [body(): lax.psum_scatter(per_device, 'ctx', scatter_dimension=0, tiled=True)]
    unnamed x104 -> x90, local copies, waits for them, and re-layouts: 10.8 us -> 9.58 us
  transfers between devices with their start and end apart: 3 -> 1, of which waited for: 2 -> 1; matrix products, arithmetic and copies ran while one was open for 22% -> 5% of each run, Pallas kernels for 20% -> 0%
where the time goes in v4:
time: 464 us; the launch traced here: 462 us
  Pallas kernels  215 us (46%)
  local copies, waits for them, and re-layouts  82 us (18%)
  blocking collectives  62.2 us (13%)
  matrix products  47.5 us (10%)
  other arithmetic  27.3 us (6%)
  between operations  18.5 us (4%)
  waiting for transfers between devices  9.2 us (2%)
    pallas_call x1, Pallas kernels, exchange(): pl.pallas_call(lambda *refs: exchange_kernel(n_ctx, n_wt, *refs), out_sha...  55.5 us
    pallas_call x1, Pallas kernels, gather_wt(): pl.pallas_call(lambda *refs: gather_kernel(n_wt, count, scattered, *refs)...  47.2 us
    pallas_call x1, Pallas kernels, unpack_weights(): pl.pallas_call(lambda *refs: unpack_kernel(parts, *refs), out_shape=(jax....  47 us
    pallas_call x1, Pallas kernels, reduce_attention(): pl.pallas_call(lambda *refs: reduce_kernel(n_ctx, n_wt, owners, *refs), o...  43.8 us
    all_gather x1, blocking collectives, body(): lax.all_gather(normed_two, 'wt', axis=0, tiled=True)  29 us
    pad x1, local copies, waits for them, and re-layouts, body(): jnp.pad(params, ((0, 0), (0, -shard_len % 1024 + 10240))).reshape(-1, LANES)  23.4 us
    all_gather x1, blocking collectives, body(): lax.all_gather(cot_bf, 'wt', axis=0, tiled=True)  23.2 us
    pallas_call x1, Pallas kernels, assemble(): pl.pallas_call(lambda *refs: assemble_kernel(parts, row_of_small, *refs),...  21.6 us
  transfers between devices with their start and end apart: 1, of which 1 were waited for; matrix products, arithmetic and copies ran while one was open for 5% of the time, Pallas kernels for 0%

profile of v4, /device:TPU:0, one launch (start us, length us, event | category | flops | bytes accessed | tf_op | source)
XLA Modules:
  0.0 462.4 jit_solution(9951764587093770638)
XLA Ops:
  16.1 23.2 %all_gather.11 = bf16[512,896]{1,0:T(8,128)(2,1)} all-gather(bf16[128,896]{1,0:T(8,128)(2,1)S(1)} %bitcast_convert_fusion), channel_id=1, replica_groups=mesh['ctx'=8,'wt'=4] {'wt'}, dimensions={0}, use_global_device_ids=true | all-gather | bytes 1146880 | tf_op jit(solution)/shard_map/all_gather | solution.py:870
  39.4 23.4 %pad.38 = f32[1,3738624]{1,0:T(1,128)} pad(f32[1,3728096]{1,0:T(1,128)} %param.24, f32[]{:T(128)} %constant.273.clone.1), padding=0_0x0_10528 | pad | bytes 29866884 | tf_op jit(solution)/shard_map/jit(_pad)/pad | solution.py:738
  62.7 47.0 %shard_map.127 = (bf16[4,224,2048]{2,1,0:T(8,128)(2,1)}, bf16[4,5,16,128]{3,2,1,0:T(8,128)(2,1)}, bf16[1216,896]{1,0:T(8,128)(2,1)}, bf16[1216,896]{1,0:T(8,128)(2,1)}, bf16[1216,896]{1,0:T(8,128)(2,1)}) custom-call(f32[29208,128]{1,0:T(8,128)} %bitcast.507), custom_call_target="tpu_custom_call" | custom-call | tf_op jit(solution)/shard_map/pallas_call | solution.py:279
  116.0 10.0 %all_gather.9 = bf16[1024,256]{0,1:T(8,128)(2,1)S(1)} all-gather(bf16[128,256]{0,1:T(8,128)(2,1)S(1)} %pad_maximum_fusion.5), channel_id=1, replica_groups=mesh['ctx'=8,'wt'=4] {'ctx'}, dimensions={0}, use_global_device_ids=true | all-gather | bytes 589824 | tf_op jit(solution)/shard_map/all_gather | solution.py:773
  126.3 3.9 gather_fusion
  134.6 2.4 while.76
  142.4 29.0 %all_gather.10 = bf16[512,896]{1,0:T(8,128)(2,1)S(1)} all-gather(bf16[128,896]{1,0:T(8,128)(2,1)S(1)} %multiply_convert_fusion.4), channel_id=1, replica_groups=mesh['ctx'=8,'wt'=4] {'wt'}, dimensions={0}, use_global_device_ids=true | all-gather | bytes 1146880 | tf_op jit(solution)/shard_map/all_gather | solution.py:869
  174.8 2.5 multiply_convert_fusion
  180.3 2.8 fusion.150
  187.3 2.8 convolution_add_fusion
  198.3 55.5 %shard_map.128 = (f32[128,896]{1,0:T(8,128)}, f32[128,896]{1,0:T(8,128)}, bf16[4,544,896]{2,1,0:T(8,128)(2,1)}) custom-call(f32[4,128,896]{2,1,0:T(8,128)} %bitcast.537, f32[4,128,896]{2,1,0:T(8,128)} %bitcast.557, bf16[8,544,896]{2,1,0:T(8,128)(2,1)} %fusion.83.refs_2_), custom_call_target="tpu_custom_call" | custom-call | tf_op jit(solution)/shard_map/pallas_call | solution.py:707
  255.7 2.3 fusion.137
  260.9 4.0 while.78
  265.0 8.0 %while.79 = (s32[]{:T(128)}, f32[64,2,7,64]{0,3,2,1:T(8,128)S(1)}, f32[1024,256]{0,1:T(8,128)S(1)}, s32[]{:T(128)}, bf16[1024,256]{0,1:T(8,128)(2,1)S(1)}, /*ind...) while((s32[]{:T(128)}, f32[64,2,7,64]{0,3,2,1:T(8,128)S(1)}, ...), condition=%wide.region_23.24_spmd.clone, body=%wide.region_22.23_spmd.clone.sunk | while | flops 297747008 | bytes 12726007 | solution.py:966
  273.7 3.5 gather_fusion.1
  289.4 5.0 %pad.46 = f32[1,466944]{1,0:T(1,128)} pad(f32[1,466012]{1,0:T(1,128)} %param.25, f32[]{:T(128)} %constant.273.clone.1), padding=0_0x0_932 | pad | bytes 3731828 | tf_op jit(solution)/shard_map/jit(_pad)/pad | solution.py:1081
  294.4 3.4 pad.47
  301.4 3.0 constant_dynamic-slice_fusion.6.refs_4_
  304.4 9.2 %reduce-scatter.2.cloned.1.call-done = f32[128,256]{1,0:T(8,128)} async-done(((f32[1024,256]{1,0:T(8,128)}), f32[128,256]{1,0:T(8,128)}) %reduce-scatter.2.cloned.1.call-update) | async-done | bytes 131088 | tf_op jit(solution)/shard_map/reduce_scatter | solution.py:995
  321.4 47.2 %shard_map.129 = (bf16[4,128,224]{2,1,0:T(8,128)(2,1)}, bf16[4,128,224]{2,1,0:T(8,128)(2,1)}, bf16[4,128,896]{2,1,0:T(8,128)(2,1)}, bf16[4,128,896]{2,1,0:T(8,128)(2,1)}, bf16[4,128,256]{2,1,0:T(8,128)(2,1)}) custom-call(bf16[4,128,224]{2,1,0:T(8,128)(2,1)} %fusion.107.refs_0_, bf16[4,128,224]{2,1,0:T(8,128)(2,1)} %maximum_bitcast_fusion.refs_1_, ...), custom_call_target="tpu_custom_call" | custom-call | tf_op jit(solution)/shard_map/pallas_call | solution.py:342
  374.4 43.8 %shard_map.130 = (f32[8,28,2048]{2,1,0:T(8,128)}, f32[24,128]{1,0:T(8,128)}) custom-call(bf16[8,28,2048]{2,1,0:T(8,128)(2,1)} %pad_maximum_fusion.refs_0_, f32[24,128]{1,0:T(8,128)} %pad_bitcast_fusion.refs_1_), custom_call_target="tpu_custom_call" | custom-call | tf_op jit(solution)/shard_map/pallas_call | solution.py:448
  420.0 2.8 reshape.542.refs_2_
  423.5 21.6 %shard_map.131 = (f32[3648,128]{1,0:T(8,128)}, f32[3648,128]{1,0:T(8,128)}, f32[3648,128]{1,0:T(8,128)}, f32[3648,128]{1,0:T(8,128)}) custom-call(s32[5]{0:T(128)} %stack.56.refs_0_, f32[16,128]{1,0:T(8,128)} %pad.45.refs_1_, f32[224,2048]{1,0:T(8,128)} %reshape.542.refs_2_, bf16[4,544,896]{2,1,0:T(8,128)(2,1)} %get-tuple-element.311.refs_3_, ...), custom_call_target="tpu_custom_call" | custom-call | tf_op jit(solution)/shard_map/pallas_call | solution.py:591
  445.1 3.8 slice.246
  (317 shorter events, 101.9 us)
Async XLA Ops:
  7.2 306.4 %reduce-scatter.2.cloned.1.call-start = ((), (), s32[]{:S(2)}) async-start(), calls=%async_computation.1 | async-start | bytes 1179648 | tf_op jit(solution)/shard_map/reduce_scatter | solution.py:995
  14.3 96.9 %copy-start.32 = (f32[128]{0:T(128)}, f32[128]{0:T(128)S(1)}, u32[]{:S(2)}) copy-start(f32[128]{0:T(128)S(1)} %get-tuple-element.737) | copy-start | bytes 1540
  62.7 48.5 %copy-start = (f32[1,128,896]{2,1,0:T(8,128)S(1)}, f32[1,128,896]{2,1,0:T(8,128)}, u32[]{:S(2)}) copy-start(f32[1,128,896]{2,1,0:T(8,128)} %param.20) | copy-start | bytes 1376260
  130.9 3.5 copy-start.1
  133.8 5.7 %copy-start.5 = (f32[2,7,64,64]{3,2,1,0:T(8,128)}, f32[2,7,64,64]{3,2,1,0:T(8,128)S(1)}, u32[]{:S(2)}) copy-start(f32[2,7,64,64]{3,2,1,0:T(8,128)S(1)} %get-tuple-element.291) | copy-start | bytes 688132
  140.2 31.2 %copy-start.37 = (bf16[1216,896]{1,0:T(8,128)(2,1)S(1)}, bf16[1216,896]{1,0:T(8,128)(2,1)}, u32[]{:S(2)}) copy-start(bf16[1216,896]{1,0:T(8,128)(2,1)} %get-tuple-element.296) | copy-start | bytes 6537220
  173.0 1.8 copy-start.20
  198.3 57.3 %copy-start.17 = (f32[1,128,896]{2,1,0:T(8,128)S(1)}, f32[1,128,896]{2,1,0:T(8,128)}, u32[]{:S(2)}) copy-start(f32[1,128,896]{2,1,0:T(8,128)} %param.21) | copy-start | bytes 1376260
  257.9 2.3 copy-start.11
  260.9 4.1 copy-start.31
  273.7 3.5 copy-start.34
  277.1 2.2 copy-start.8
  289.4 5.0 %copy-start.13 = (f32[1,466012]{1,0:T(1,128)S(1)}, f32[1,466012]{1,0:T(1,128)}, u32[]{:S(2)}) copy-start(f32[1,466012]{1,0:T(1,128)} %param.26) | copy-start | bytes 5592148
  294.4 4.0 copy-start.21
  294.4 4.0 copy-start.22
  294.4 4.8 %copy-start.33 = (f32[128]{0:T(128)S(1)}, f32[128]{0:T(128)}, u32[]{:S(2)}) copy-start(f32[128]{0:T(128)} %copy-done.32) | copy-start | bytes 1540
  301.4 17.2 %copy-start.12 = (bf16[128,896]{1,0:T(8,128)(2,1)}, bf16[128,896]{1,0:T(8,128)(2,1)S(1)}, u32[]{:S(2)}) copy-start(bf16[128,896]{1,0:T(8,128)(2,1)S(1)} %add_convert_fusion.refs_3_) | copy-start | bytes 688132
  301.4 13.3 %copy-start.23 = (f32[128,128]{1,0:T(8,128)S(1)}, f32[128,128]{1,0:T(8,128)}, u32[]{:S(2)}) copy-start(f32[128,128]{1,0:T(8,128)} %copy.110) | copy-start | bytes 196612
  318.6 2.1 copy-start.27
  318.6 2.2 copy-start.24
  368.6 3.2 copy-start.19
  445.1 3.8 copy-start.16
  448.9 2.0 copy-start.15
  450.9 2.0 copy-start.14
  (16 other events, 18.7 us)
Sparse Core Ops, SparseCore 0:
  278.5 35.0 reduce-scatter.1
